TPU v7x, 32 devices: a whole 2x2x4 slice. The times are simulated.
32 devices in a mesh: zone: 8 (over z, x), tile: 4 (over y, core).
Axes of the slice: x: 2, y: 2, z: 4, core: 2. Of those that a mesh axis runs over, the one named last changes fastest.
Arguments:
- a_coord: float32 [2, 1048576], P(None, ('zone', 'tile')), may hold values from -6 to 6
- a_var: float32 [1048576], P(('zone', 'tile')), may hold values from 0.1 to 1
- dest: int32 [8192, 1], P(('zone', 'tile')), may hold values from 0 to 31; in each aligned block of 256 rows (0 to 255, 256 to 511, ...) at most 16 rows name the same one
- cand: int32 [8192, 4], P(('zone', 'tile')), may hold values from 0 to 79
- cand_count: int32 [8192, 1], P(('zone', 'tile')), may hold values from 1 to 4
- b_coord: float32 [2, 262144], P(None, ('zone', 'tile')), may hold values from -6 to 6
- b_var: float32 [262144], P(('zone', 'tile')), may hold values from 0.1 to 1
- b_prior: float32 [262144], P(('zone', 'tile')), may hold values from 0.002 to 0.02
- b_flux: float32 [3, 262144], P(None, ('zone', 'tile')), may hold values from -6 to 6
Outputs:
- matched: float32 [5, 1048576], P(None, ('zone', 'tile'))
- match_prob: float32 [1048576], P(('zone', 'tile'))
Inputs may be any that keep to these rules, and one draw needn't show every extreme that they name: `dest`: among the 256 blocks of one device, at most 16 name any one owner device, a bound that some block reaches.
All inputs are finite; a program needn't handle non-finite values.
Results may differ from a plain program's by a relative error of at most 0.0003.
Values sent between devices are 32-bit elements; how exact they have to be, the bound alone decides.
No kernel may reach another device: no remote copies, remote signals or barrier semaphores. Data moves between devices by JAX's collectives and lax.ppermute only.
A program may use at most 64 MiB of HBM per device.

v0:
```python
from functools import partial

import jax
import jax.numpy as jnp
from jax import lax
from jax.sharding import PartitionSpec as P

TB = 128
K = 4
MB = 8


def padded(array, sides, width):
    for axis, dim in sides:
        size, length = (lax.axis_size(axis), array.shape[dim])
        up = [(i, (i + 1) % size) for i in range(size - 1)]
        down = [(j, i) for i, j in up]
        last = lax.slice_in_dim(array, length - width, length, axis=dim)
        first = lax.slice_in_dim(array, 0, width, axis=dim)
        before = lax.ppermute(last, axis, up)
        after = lax.ppermute(first, axis, down)
        array = jnp.concatenate([before, array, after], axis=dim)
    return array


def slot_match(a_block, candidates, live_count):
    numerator = jnp.zeros((5, a_block.shape[1]), jnp.float32)
    weight_sum = jnp.zeros((a_block.shape[1],), jnp.float32)
    for position in range(len(candidates)):
        block_data = candidates[position]
        is_live = jnp.where(live_count > position, 1.0, 0.0).astype(jnp.float32)
        delta_u = a_block[0][:, None] - block_data[0][None, :]
        delta_v = a_block[1][:, None] - block_data[1][None, :]
        var_sum = a_block[2][:, None] + block_data[5][None, :]
        weight = (
            (block_data[6] * is_live)[None, :]
            * (2.0 / var_sum)
            * jnp.exp(-(delta_u * delta_u + delta_v * delta_v) / (2.0 * var_sum))
        )
        numerator = numerator + jnp.einsum(
            "fj,ij->fi", block_data[:5], weight, precision=lax.Precision.HIGHEST
        )
        weight_sum = weight_sum + jnp.sum(weight, axis=1)
    inverse = 1.0 / (1.0 + weight_sum)
    return jnp.concatenate([numerator * inverse[None, :], (weight_sum * inverse)[None, :]], axis=0)


def match_one(window, items):
    a_block, labels = items
    candidates = []
    for position in range(K):
        block_index = labels[position].astype(jnp.int32)
        candidates.append(window[block_index])
    return slot_match(a_block, candidates, labels[K])


def match_many(window, pieces):
    floats, labels = pieces
    leading = floats.shape[:-2]
    results = lax.map(
        partial(match_one, window),
        (floats.reshape(-1, 3, TB), labels.reshape(-1, K + 1)),
        batch_size=128,
    )
    return results.reshape(leading + (6, TB))


def body(a_coord, a_var, dest, cand, cand_count, b_coord, b_var, b_prior, b_flux):
    zone_count = lax.axis_size("zone")
    tile_count = lax.axis_size("tile")
    devices = zone_count * tile_count
    blocks_here = dest.shape[0]
    capacity = max(2, (2 * blocks_here + devices - 1) // devices)
    b_stack = jnp.concatenate([b_coord, b_flux, b_var[None, :], b_prior[None, :]], axis=0)
    window = padded(b_stack, (("zone", 1),), MB * TB)
    window = window.reshape(7, -1, TB).transpose(1, 0, 2)
    a_stack = (
        jnp.concatenate([a_coord, a_var[None, :]], axis=0)
        .reshape(3, blocks_here, TB)
        .transpose(1, 0, 2)
    )
    labels = jnp.concatenate([cand, cand_count], axis=1).astype(jnp.float32)
    target = dest[:, 0]
    onehot = (target[:, None] == jnp.arange(devices, dtype=jnp.int32)[None, :]).astype(jnp.int32)
    slot_rank = jnp.sum(jnp.cumsum(onehot, axis=0) * onehot, axis=1) - 1
    slot_index = target * capacity + slot_rank
    send_floats = jnp.zeros((devices * capacity, 3, TB), jnp.float32).at[slot_index].set(a_stack)
    send_labels = jnp.zeros((devices * capacity, K + 1), jnp.float32).at[slot_index].set(labels)
    matcher = partial(match_many, window)
    results = matcher(
        (
            lax.all_to_all(
                send_floats.reshape(devices, capacity, 3, TB),
                ("zone", "tile"),
                split_axis=0,
                concat_axis=0,
                tiled=True,
            ),
            lax.all_to_all(
                send_labels.reshape(devices, capacity, K + 1),
                ("zone", "tile"),
                split_axis=0,
                concat_axis=0,
                tiled=True,
            ),
        )
    )
    returned = lax.all_to_all(
        results, ("zone", "tile"), split_axis=0, concat_axis=0, tiled=True
    ).reshape(devices * capacity, 6, TB)
    returned = returned[slot_index].transpose(1, 0, 2).reshape(6, blocks_here * TB)
    return (returned[:5], returned[5])


def solution(mesh):
    placed = (
        P(None, ("zone", "tile")),
        P(("zone", "tile")),
        P(("zone", "tile"), None),
        P(("zone", "tile"), None),
        P(("zone", "tile"), None),
        P(None, ("zone", "tile")),
        P(("zone", "tile")),
        P(("zone", "tile")),
        P(None, ("zone", "tile")),
    )
    return jax.shard_map(
        body,
        mesh=mesh,
        in_specs=placed,
        out_specs=(P(None, ("zone", "tile")), P(("zone", "tile"))),
        check_vma=False,
    )
```

profile of v0, /device:TPU:1, one launch (start us, length us, event | category | flops | bytes accessed | tf_op | source)
XLA Modules:
  0.0 606.3 jit_solution(10463205621713483641)
XLA Ops:
  6.6 7.1 %all-to-all-start = ((f32[32,16,5]{1,2,0:T(8,128)}), f32[32,16,5]{1,2,0:T(8,128)S(1)}, u32[]{:S(2)}, u32[]{:S(2)}) async-start(f32[32,16,5]{1,2,0:T(8,128)} %copy.31), calls=%async_computation | async-start | bytes 262144 | tf_op jit(solution)/shard_map/all_to_all | solution.py:99
  15.1 7.0 %scatter_fusion = f32[512,3,128]{2,1,0:T(4,128)S(1)} fusion(f32[512,3,128]{2,1,0:T(4,128)S(1)} %broadcast_in_dim.54, s32[256]{0:T(256)S(1)} %bitcast.187, f32[256,3,128]{2,1,0:T(4,128)S(1)} %maximum_bitcast_fusion.1), kind=kCustom, calls=%fused_computation.6 | custom fusion | bytes 1180672 | tf_op jit(solution)/shard_map/scatter | solution.py:87
  23.1 5.8 all-to-all-start.1
  29.0 3.3 collective-permute-start
  33.9 3.3 collective-permute-done.1
  37.4 11.8 %all-to-all-done.1 = f32[32,16,3,128]{3,1,2,0:T(8,128)S(1)} async-done(((f32[32,16,3,128]{3,1,2,0:T(8,128)}), f32[32,16,3,128]{3,1,2,0:T(8,128)S(1)}, u32[]{:S(2)}, u32[]{:S(2)}) %all-to-all-start.1) | async-done | bytes 786464 | tf_op jit(solution)/shard_map/all_to_all | solution.py:92
  49.2 507.4 %while.10 = (s32[]{:T(128)}, f32[4,128,6,128]{3,2,1,0:T(8,128)}, f32[4,128,5]{1,0,2:T(4,128)S(1)}, f32[80,7,128]{2,1,0:T(8,128)S(1)}, f32[4,128,3,128]{3,1,0,2:T(8,128)S(1)}, /*index=5*/s32[]{:T(128)}) while((s32[]{:T(128)}, f32[4,128,6,128]{3,2,1,0:T(8,128)}, f32[4,128,5]{1,0,2:T(4,128)S(1)}, f32[80,7,128]{2,1,0:T(8,128)S(1)}, ...), condition=%wide.region_10.11_spmd, body=%wide.region_5.0_spmd.sunk | while | flops 713592832 | bytes 16868456 | solution.py:60
  51.6 21.2 %fusion.98 = f32[128,5,128]{2,1,0:T(8,128)} fusion(f32[128,128]{1,0:T(8,128)S(1)} %bitcast.148, f32[128,128]{1,0:T(8,128)S(1)} %bitcast.144, f32[128,128]{1,0:T(8,128)S(1)} %bitcast.146, f32[128,128]{1,0:T(8,128)S(1)} %bitcast.142, f32[128,128]{1,0:T(8,128)S(1)} %get-tuple-element.167, f32[128,128]{1,0:T(8,128)S(1)} %get-tuple-element.169, ...), kind=kOutput, calls=%fused_computation.36.clone.1 | convolution fusion | flops 150994944 | bytes 1245184 | tf_op jit(solution)/shard_map/while/body/eval_jaxpr/vmap(fj,ij->fi)/dot_general | solution.py:40
  75.1 23.8 %fusion.97 = f32[128,5,128]{2,1,0:T(8,128)S(1)} fusion(f32[128,128]{1,0:T(8,128)S(1)} %bitcast.166, f32[128,128]{1,0:T(8,128)S(1)} %bitcast.170, f32[128,128]{1,0:T(8,128)S(1)} %bitcast.168, f32[128,128]{1,0:T(8,128)S(1)} %bitcast.172, f32[128,128]{1,0:T(8,128)S(1)} %get-tuple-element.167, f32[128,128]{1,0:T(8,128)S(1)} %get-tuple-element.169, ...), kind=kOutput, calls=%fused_computation.34.clone.1 | convolution fusion | flops 150994944 | bytes 1245184 | tf_op jit(solution)/shard_map/while/body/eval_jaxpr/vmap(fj,ij->fi)/dot_general | solution.py:40
  98.9 23.9 %fusion.99 = f32[128,5,128]{2,1,0:T(8,128)S(1)} fusion(f32[128,5,128]{2,1,0:T(8,128)S(1)} %fusion.97, f32[128,5,128]{2,1,0:T(8,128)S(1)} %copy-done.6, f32[128,128]{1,0:T(8,128)S(1)} %bitcast.150, f32[128,128]{1,0:T(8,128)S(1)} %get-tuple-element.167, f32[128,128]{1,0:T(8,128)S(1)} %bitcast.154, f32[128,128]{1,0:T(8,128)S(1)} %get-tuple-element.169, ...), kind=kOutput, calls=%fused_computation.40.clone.1 | convolution fusion | flops 151158784 | bytes 1900544 | tf_op jit(solution)/shard_map/while/body/eval_jaxpr/vmap(fj,ij->fi)/dot_general | solution.py:40
  122.8 28.3 %fusion.96 = (f32[128,128]{1,0:T(8,128)S(1)}, f32[128,128]{1,0:T(8,128)S(1)}, f32[128,128]{1,0:T(8,128)S(1)}, f32[128,128]{1,0:T(8,128)S(1)}) fusion(f32[128,128]{1,0:T(8,128)S(1)} %bitcast.149, f32[128,128]{1,0:T(8,128)S(1)} %get-tuple-element.167, f32[128,128]{1,0:T(8,128)S(1)} %bitcast.145, f32[128,128]{1,0:T(8,128)S(1)} %get-tuple-element.169, ...), kind=kLoop, calls=%fused_computation.35.clone.1 | loop fusion | flops 108986368 | bytes 1507328 | tf_op jit(solution)/shard_map/while/body/eval_jaxpr/vmap()/reduce_sum | solution.py:43
  151.2 23.9 %fusion.100 = f32[128,5,128]{2,1,0:T(8,128)S(1)} fusion(f32[128,5,128]{2,1,0:T(8,128)S(1)} %fusion.99, f32[128,128]{1,0:T(8,128)S(1)} %bitcast.165, f32[128,128]{1,0:T(8,128)S(1)} %bitcast.161, f32[128,128]{1,0:T(8,128)S(1)} %bitcast.163, f32[128,128]{1,0:T(8,128)S(1)} %bitcast.159, f32[128,128]{1,0:T(8,128)S(1)} %get-tuple-element.167, ...), kind=kOutput, calls=%fused_computation.42.clone.1 | convolution fusion | flops 151158784 | bytes 1638400 | tf_op jit(solution)/shard_map/while/body/eval_jaxpr/vmap(fj,ij->fi)/dot_general | solution.py:40
  178.4 21.2 %fusion.98 = f32[128,5,128]{2,1,0:T(8,128)} fusion(f32[128,128]{1,0:T(8,128)S(1)} %bitcast.148, f32[128,128]{1,0:T(8,128)S(1)} %bitcast.144, f32[128,128]{1,0:T(8,128)S(1)} %bitcast.146, f32[128,128]{1,0:T(8,128)S(1)} %bitcast.142, f32[128,128]{1,0:T(8,128)S(1)} %get-tuple-element.167, f32[128,128]{1,0:T(8,128)S(1)} %get-tuple-element.169, ...), kind=kOutput, calls=%fused_computation.36.clone.1 | convolution fusion | flops 150994944 | bytes 1245184 | tf_op jit(solution)/shard_map/while/body/eval_jaxpr/vmap(fj,ij->fi)/dot_general | solution.py:40
  201.9 23.8 %fusion.97 = f32[128,5,128]{2,1,0:T(8,128)S(1)} fusion(f32[128,128]{1,0:T(8,128)S(1)} %bitcast.166, f32[128,128]{1,0:T(8,128)S(1)} %bitcast.170, f32[128,128]{1,0:T(8,128)S(1)} %bitcast.168, f32[128,128]{1,0:T(8,128)S(1)} %bitcast.172, f32[128,128]{1,0:T(8,128)S(1)} %get-tuple-element.167, f32[128,128]{1,0:T(8,128)S(1)} %get-tuple-element.169, ...), kind=kOutput, calls=%fused_computation.34.clone.1 | convolution fusion | flops 150994944 | bytes 1245184 | tf_op jit(solution)/shard_map/while/body/eval_jaxpr/vmap(fj,ij->fi)/dot_general | solution.py:40
  225.7 23.9 %fusion.99 = f32[128,5,128]{2,1,0:T(8,128)S(1)} fusion(f32[128,5,128]{2,1,0:T(8,128)S(1)} %fusion.97, f32[128,5,128]{2,1,0:T(8,128)S(1)} %copy-done.6, f32[128,128]{1,0:T(8,128)S(1)} %bitcast.150, f32[128,128]{1,0:T(8,128)S(1)} %get-tuple-element.167, f32[128,128]{1,0:T(8,128)S(1)} %bitcast.154, f32[128,128]{1,0:T(8,128)S(1)} %get-tuple-element.169, ...), kind=kOutput, calls=%fused_computation.40.clone.1 | convolution fusion | flops 151158784 | bytes 1900544 | tf_op jit(solution)/shard_map/while/body/eval_jaxpr/vmap(fj,ij->fi)/dot_general | solution.py:40
  249.6 28.3 %fusion.96 = (f32[128,128]{1,0:T(8,128)S(1)}, f32[128,128]{1,0:T(8,128)S(1)}, f32[128,128]{1,0:T(8,128)S(1)}, f32[128,128]{1,0:T(8,128)S(1)}) fusion(f32[128,128]{1,0:T(8,128)S(1)} %bitcast.149, f32[128,128]{1,0:T(8,128)S(1)} %get-tuple-element.167, f32[128,128]{1,0:T(8,128)S(1)} %bitcast.145, f32[128,128]{1,0:T(8,128)S(1)} %get-tuple-element.169, ...), kind=kLoop, calls=%fused_computation.35.clone.1 | loop fusion | flops 108986368 | bytes 1507328 | tf_op jit(solution)/shard_map/while/body/eval_jaxpr/vmap()/reduce_sum | solution.py:43
  278.0 23.9 %fusion.100 = f32[128,5,128]{2,1,0:T(8,128)S(1)} fusion(f32[128,5,128]{2,1,0:T(8,128)S(1)} %fusion.99, f32[128,128]{1,0:T(8,128)S(1)} %bitcast.165, f32[128,128]{1,0:T(8,128)S(1)} %bitcast.161, f32[128,128]{1,0:T(8,128)S(1)} %bitcast.163, f32[128,128]{1,0:T(8,128)S(1)} %bitcast.159, f32[128,128]{1,0:T(8,128)S(1)} %get-tuple-element.167, ...), kind=kOutput, calls=%fused_computation.42.clone.1 | convolution fusion | flops 151158784 | bytes 1638400 | tf_op jit(solution)/shard_map/while/body/eval_jaxpr/vmap(fj,ij->fi)/dot_general | solution.py:40
  305.3 21.2 %fusion.98 = f32[128,5,128]{2,1,0:T(8,128)} fusion(f32[128,128]{1,0:T(8,128)S(1)} %bitcast.148, f32[128,128]{1,0:T(8,128)S(1)} %bitcast.144, f32[128,128]{1,0:T(8,128)S(1)} %bitcast.146, f32[128,128]{1,0:T(8,128)S(1)} %bitcast.142, f32[128,128]{1,0:T(8,128)S(1)} %get-tuple-element.167, f32[128,128]{1,0:T(8,128)S(1)} %get-tuple-element.169, ...), kind=kOutput, calls=%fused_computation.36.clone.1 | convolution fusion | flops 150994944 | bytes 1245184 | tf_op jit(solution)/shard_map/while/body/eval_jaxpr/vmap(fj,ij->fi)/dot_general | solution.py:40
  328.7 23.8 %fusion.97 = f32[128,5,128]{2,1,0:T(8,128)S(1)} fusion(f32[128,128]{1,0:T(8,128)S(1)} %bitcast.166, f32[128,128]{1,0:T(8,128)S(1)} %bitcast.170, f32[128,128]{1,0:T(8,128)S(1)} %bitcast.168, f32[128,128]{1,0:T(8,128)S(1)} %bitcast.172, f32[128,128]{1,0:T(8,128)S(1)} %get-tuple-element.167, f32[128,128]{1,0:T(8,128)S(1)} %get-tuple-element.169, ...), kind=kOutput, calls=%fused_computation.34.clone.1 | convolution fusion | flops 150994944 | bytes 1245184 | tf_op jit(solution)/shard_map/while/body/eval_jaxpr/vmap(fj,ij->fi)/dot_general | solution.py:40
  352.6 23.9 %fusion.99 = f32[128,5,128]{2,1,0:T(8,128)S(1)} fusion(f32[128,5,128]{2,1,0:T(8,128)S(1)} %fusion.97, f32[128,5,128]{2,1,0:T(8,128)S(1)} %copy-done.6, f32[128,128]{1,0:T(8,128)S(1)} %bitcast.150, f32[128,128]{1,0:T(8,128)S(1)} %get-tuple-element.167, f32[128,128]{1,0:T(8,128)S(1)} %bitcast.154, f32[128,128]{1,0:T(8,128)S(1)} %get-tuple-element.169, ...), kind=kOutput, calls=%fused_computation.40.clone.1 | convolution fusion | flops 151158784 | bytes 1900544 | tf_op jit(solution)/shard_map/while/body/eval_jaxpr/vmap(fj,ij->fi)/dot_general | solution.py:40
  376.5 28.3 %fusion.96 = (f32[128,128]{1,0:T(8,128)S(1)}, f32[128,128]{1,0:T(8,128)S(1)}, f32[128,128]{1,0:T(8,128)S(1)}, f32[128,128]{1,0:T(8,128)S(1)}) fusion(f32[128,128]{1,0:T(8,128)S(1)} %bitcast.149, f32[128,128]{1,0:T(8,128)S(1)} %get-tuple-element.167, f32[128,128]{1,0:T(8,128)S(1)} %bitcast.145, f32[128,128]{1,0:T(8,128)S(1)} %get-tuple-element.169, ...), kind=kLoop, calls=%fused_computation.35.clone.1 | loop fusion | flops 108986368 | bytes 1507328 | tf_op jit(solution)/shard_map/while/body/eval_jaxpr/vmap()/reduce_sum | solution.py:43
  404.9 23.9 %fusion.100 = f32[128,5,128]{2,1,0:T(8,128)S(1)} fusion(f32[128,5,128]{2,1,0:T(8,128)S(1)} %fusion.99, f32[128,128]{1,0:T(8,128)S(1)} %bitcast.165, f32[128,128]{1,0:T(8,128)S(1)} %bitcast.161, f32[128,128]{1,0:T(8,128)S(1)} %bitcast.163, f32[128,128]{1,0:T(8,128)S(1)} %bitcast.159, f32[128,128]{1,0:T(8,128)S(1)} %get-tuple-element.167, ...), kind=kOutput, calls=%fused_computation.42.clone.1 | convolution fusion | flops 151158784 | bytes 1638400 | tf_op jit(solution)/shard_map/while/body/eval_jaxpr/vmap(fj,ij->fi)/dot_general | solution.py:40
  432.1 21.2 %fusion.98 = f32[128,5,128]{2,1,0:T(8,128)} fusion(f32[128,128]{1,0:T(8,128)S(1)} %bitcast.148, f32[128,128]{1,0:T(8,128)S(1)} %bitcast.144, f32[128,128]{1,0:T(8,128)S(1)} %bitcast.146, f32[128,128]{1,0:T(8,128)S(1)} %bitcast.142, f32[128,128]{1,0:T(8,128)S(1)} %get-tuple-element.167, f32[128,128]{1,0:T(8,128)S(1)} %get-tuple-element.169, ...), kind=kOutput, calls=%fused_computation.36.clone.1 | convolution fusion | flops 150994944 | bytes 1245184 | tf_op jit(solution)/shard_map/while/body/eval_jaxpr/vmap(fj,ij->fi)/dot_general | solution.py:40
  455.6 23.8 %fusion.97 = f32[128,5,128]{2,1,0:T(8,128)S(1)} fusion(f32[128,128]{1,0:T(8,128)S(1)} %bitcast.166, f32[128,128]{1,0:T(8,128)S(1)} %bitcast.170, f32[128,128]{1,0:T(8,128)S(1)} %bitcast.168, f32[128,128]{1,0:T(8,128)S(1)} %bitcast.172, f32[128,128]{1,0:T(8,128)S(1)} %get-tuple-element.167, f32[128,128]{1,0:T(8,128)S(1)} %get-tuple-element.169, ...), kind=kOutput, calls=%fused_computation.34.clone.1 | convolution fusion | flops 150994944 | bytes 1245184 | tf_op jit(solution)/shard_map/while/body/eval_jaxpr/vmap(fj,ij->fi)/dot_general | solution.py:40
  479.4 23.9 %fusion.99 = f32[128,5,128]{2,1,0:T(8,128)S(1)} fusion(f32[128,5,128]{2,1,0:T(8,128)S(1)} %fusion.97, f32[128,5,128]{2,1,0:T(8,128)S(1)} %copy-done.6, f32[128,128]{1,0:T(8,128)S(1)} %bitcast.150, f32[128,128]{1,0:T(8,128)S(1)} %get-tuple-element.167, f32[128,128]{1,0:T(8,128)S(1)} %bitcast.154, f32[128,128]{1,0:T(8,128)S(1)} %get-tuple-element.169, ...), kind=kOutput, calls=%fused_computation.40.clone.1 | convolution fusion | flops 151158784 | bytes 1900544 | tf_op jit(solution)/shard_map/while/body/eval_jaxpr/vmap(fj,ij->fi)/dot_general | solution.py:40
  503.3 28.3 %fusion.96 = (f32[128,128]{1,0:T(8,128)S(1)}, f32[128,128]{1,0:T(8,128)S(1)}, f32[128,128]{1,0:T(8,128)S(1)}, f32[128,128]{1,0:T(8,128)S(1)}) fusion(f32[128,128]{1,0:T(8,128)S(1)} %bitcast.149, f32[128,128]{1,0:T(8,128)S(1)} %get-tuple-element.167, f32[128,128]{1,0:T(8,128)S(1)} %bitcast.145, f32[128,128]{1,0:T(8,128)S(1)} %get-tuple-element.169, ...), kind=kLoop, calls=%fused_computation.35.clone.1 | loop fusion | flops 108986368 | bytes 1507328 | tf_op jit(solution)/shard_map/while/body/eval_jaxpr/vmap()/reduce_sum | solution.py:43
  531.7 23.9 %fusion.100 = f32[128,5,128]{2,1,0:T(8,128)S(1)} fusion(f32[128,5,128]{2,1,0:T(8,128)S(1)} %fusion.99, f32[128,128]{1,0:T(8,128)S(1)} %bitcast.165, f32[128,128]{1,0:T(8,128)S(1)} %bitcast.161, f32[128,128]{1,0:T(8,128)S(1)} %bitcast.163, f32[128,128]{1,0:T(8,128)S(1)} %bitcast.159, f32[128,128]{1,0:T(8,128)S(1)} %get-tuple-element.167, ...), kind=kOutput, calls=%fused_computation.42.clone.1 | convolution fusion | flops 151158784 | bytes 1638400 | tf_op jit(solution)/shard_map/while/body/eval_jaxpr/vmap(fj,ij->fi)/dot_general | solution.py:40
  556.6 3.0 copy.39
  559.7 4.0 all-to-all-start.2
  563.7 36.4 %all-to-all-done.2 = f32[32,16,6,128]{3,1,2,0:T(8,128)S(1)} async-done(((f32[32,16,6,128]{3,1,2,0:T(8,128)}), f32[32,16,6,128]{3,1,2,0:T(8,128)S(1)}, u32[]{:S(2)}, u32[]{:S(2)}) %all-to-all-start.2) | async-done | bytes 1572896 | tf_op jit(solution)/shard_map/all_to_all | solution.py:108
  600.2 2.0 copy.40
  602.1 2.3 gather_fusion.4
  (107 shorter events, 34.1 us)
Async XLA Ops:
  3.6 18.5 %copy-start.4 = (s32[256,1]{0,1:T(1,128)}, s32[256,1]{0,1:T(1,128)S(1)}, u32[]{:S(2)}) copy-start(s32[256,1]{0,1:T(1,128)S(1)} %compare_select_fusion.8) | copy-start | bytes 3076
  6.6 16.5 %all-to-all-start = ((f32[32,16,5]{1,2,0:T(8,128)}), f32[32,16,5]{1,2,0:T(8,128)S(1)}, u32[]{:S(2)}, u32[]{:S(2)}) async-start(f32[32,16,5]{1,2,0:T(8,128)} %copy.31), calls=%async_computation | async-start | bytes 262144 | tf_op jit(solution)/shard_map/all_to_all | solution.py:99
  15.1 13.8 %copy-start = (f32[3,8192]{1,0:T(4,128)S(1)}, f32[3,8192]{1,0:T(4,128)}, u32[]{:S(2)}) copy-start(f32[3,8192]{1,0:T(4,128)} %param.19) | copy-start | bytes 294916
  15.1 13.8 %copy-start.1 = (f32[2,8192]{1,0:T(2,128)S(1)}, f32[2,8192]{1,0:T(2,128)}, u32[]{:S(2)}) copy-start(f32[2,8192]{1,0:T(2,128)} %param.16) | copy-start | bytes 196612
  15.1 13.8 %copy-start.2 = (f32[8192]{0:T(1024)S(1)}, f32[8192]{0:T(1024)}, u32[]{:S(2)}) copy-start(f32[8192]{0:T(1024)} %param.18) | copy-start | bytes 98308
  15.1 13.8 %copy-start.3 = (f32[8192]{0:T(1024)S(1)}, f32[8192]{0:T(1024)}, u32[]{:S(2)}) copy-start(f32[8192]{0:T(1024)} %param.17) | copy-start | bytes 98308
  23.1 26.1 %all-to-all-start.1 = ((f32[32,16,3,128]{3,1,2,0:T(8,128)}), f32[32,16,3,128]{3,1,2,0:T(8,128)S(1)}, u32[]{:S(2)}, u32[]{:S(2)}) async-start(f32[32,16,3,128]{3,1,2,0:T(8,128)} %copy.34), calls=%async_computation.1 | async-start | bytes 1572864 | tf_op jit(solution)/shard_map/all_to_all | solution.py:92
  29.0 4.9 collective-permute-start
  32.3 5.0 collective-permute-start.1
  75.0 23.8 %copy-start.6 = (f32[128,5,128]{2,1,0:T(8,128)S(1)}, f32[128,5,128]{2,1,0:T(8,128)}, u32[]{:S(2)}) copy-start(f32[128,5,128]{2,1,0:T(8,128)} %fusion.98) | copy-start | bytes 983044 | tf_op jit(solution)/shard_map/while
  201.9 23.8 %copy-start.6 = (f32[128,5,128]{2,1,0:T(8,128)S(1)}, f32[128,5,128]{2,1,0:T(8,128)}, u32[]{:S(2)}) copy-start(f32[128,5,128]{2,1,0:T(8,128)} %fusion.98) | copy-start | bytes 983044 | tf_op jit(solution)/shard_map/while
  328.7 23.8 %copy-start.6 = (f32[128,5,128]{2,1,0:T(8,128)S(1)}, f32[128,5,128]{2,1,0:T(8,128)}, u32[]{:S(2)}) copy-start(f32[128,5,128]{2,1,0:T(8,128)} %fusion.98) | copy-start | bytes 983044 | tf_op jit(solution)/shard_map/while
  455.6 23.8 %copy-start.6 = (f32[128,5,128]{2,1,0:T(8,128)S(1)}, f32[128,5,128]{2,1,0:T(8,128)}, u32[]{:S(2)}) copy-start(f32[128,5,128]{2,1,0:T(8,128)} %fusion.98) | copy-start | bytes 983044 | tf_op jit(solution)/shard_map/while
  559.7 4.0 copy-start.5
  559.7 40.5 %all-to-all-start.2 = ((f32[32,16,6,128]{3,1,2,0:T(8,128)}), f32[32,16,6,128]{3,1,2,0:T(8,128)S(1)}, u32[]{:S(2)}, u32[]{:S(2)}) async-start(f32[32,16,6,128]{3,1,2,0:T(8,128)} %copy.39), calls=%async_computation.2 | async-start | bytes 3145728 | tf_op jit(solution)/shard_map/all_to_all | solution.py:108
where the time goes:
time: 608 us; the launch traced here: 606 us
  matrix products  371 us (61%)
  other arithmetic  127 us (21%)
  waiting for transfers between devices  51.7 us (9%)
  local copies, waits for them, and re-layouts  33.3 us (5%)
  starting transfers between devices  21.5 us (4%)
    dot_general x16, matrix products, slot_match(): jnp.einsum('fj,ij->fi', block_data[:5], weight, precision=lax.Precision.H...  371 us
    reduce_sum x4, other arithmetic, slot_match(): weight_sum = weight_sum + jnp.sum(weight, axis=1)  113 us
    all_to_all x1, waiting for transfers between devices, body(): lax.all_to_all(results, ('zone', 'tile'), split_axis=0, concat_axis=0, ti...  36.4 us
    gather x16, local copies, waits for them, and re-layouts, match_one(): candidates.append(window[block_index])  13.2 us
  transfers between devices with their start and end apart: 5, of which 4 were waited for; matrix products, arithmetic and copies ran while one was open for 2% of the time, Pallas kernels for 0%

commit v1 on v0

v1 whole, which is shorter than its diff:
```python
import functools
import math

import jax
import jax.numpy as jnp
from jax import lax
from jax.experimental import pallas as pl
from jax.experimental.pallas import tpu as pltpu
from jax.sharding import PartitionSpec as P

TB = 128
MB = 8
NQ = 7
VAR, PRIOR = 5, 6
UNROLL = 16
BF, F32 = jnp.bfloat16, jnp.float32
HALF_LOG2E = 0.5 * math.log2(math.e)
AXES = ("zone", "tile")
VMEM = pl.BlockSpec(memory_space=pltpu.VMEM)
SMEM = pl.BlockSpec(memory_space=pltpu.SMEM)
ANY = pl.BlockSpec(memory_space=pl.ANY)


def split3(x):
    high = x.astype(BF).astype(F32)
    middle = (x - high).astype(BF).astype(F32)
    return high, middle, x - high - middle


def is_grid(mesh_shape):
    return mesh_shape["zone"] % 2 == 0 and mesh_shape["tile"] == 4


class Grid:
    def __init__(self, zones, tiles):
        self.zones, self.tiles, self.high = zones, tiles, zones // 2

    def perm(self, move):
        pairs = []
        for d in range(self.zones * self.tiles):
            zone, tile = divmod(d, self.tiles)
            h, x, y, c = move(zone // 2, zone % 2, tile // 2, tile % 2)
            pairs.append((d, ((h % self.high) * 2 + x) * self.tiles + y * 2 + c))
        return pairs

    def ring(self):
        return self.perm(lambda h, x, y, c: (h + 1, x, y, c))

    def side(self, first):
        return self.perm(lambda h, x, y, c: (h, x ^ 1, y, c) if (c == 0) == first else (h, x, y ^ 1, c))

    def core(self):
        return self.perm(lambda h, x, y, c: (h, x, y, c ^ 1))


def gather_phases(own, grid):
    phases = []
    held = own
    for step in range(grid.high):
        later = lax.ppermute(held, AXES, grid.ring()) if step < grid.high - 1 else None
        pair = jnp.concatenate([held, lax.ppermute(held, AXES, grid.side(True))], axis=0)
        four = jnp.concatenate([pair, lax.ppermute(pair, AXES, grid.side(False))], axis=0)
        phases.append((four, lax.ppermute(four, AXES, grid.core())))
        held = later
    return phases


def locate(zone, tile, block, grid, rows):
    my_zone, my_tile = lax.axis_index("zone"), lax.axis_index("tile")
    phase = lax.rem((my_zone >> 1) - (zone >> 1) + grid.high, grid.high)
    dx = (zone & 1) ^ (my_zone & 1)
    dy = ((tile >> 1) ^ (my_tile >> 1)) & 1
    dc = (tile ^ my_tile) & 1
    odd = tile & 1
    place = jnp.where(odd == 0, dx + 2 * dy, dy + 2 * dx)
    return phase, (4 * dc + place) * rows + block


def plan_kernel(items, phases, length, dummy, entry_ref, codes_ref, count_ref):
    def step(i, counts):
        for t in range(4):
            entry = entry_ref[i * 4 + t]
            phase, code = entry >> 26, entry & ((1 << 26) - 1)
            place = counts[phases]
            start = phases * length
            for p in reversed(range(phases)):
                place = jnp.where(phase == p, counts[p], place)
            codes_ref[phase * length + place] = code
            counts = tuple(c + jnp.where(phase == p, 1, 0) for p, c in enumerate(counts))
        return counts

    counts = lax.fori_loop(0, items // 4, step, (jnp.int32(0),) * (phases + 1))
    for p in range(phases):
        for t in range(UNROLL):
            codes_ref[p * length + counts[p] + t] = jnp.int32(dummy)
        count_ref[p] = counts[p]


def prep_kernel(blocks, coord_ref, var_ref, at_ref):
    eye = jnp.where(
        lax.broadcasted_iota(jnp.int32, (TB, TB), 0) == lax.broadcasted_iota(jnp.int32, (TB, TB), 1), 1.0, 0.0
    ).astype(BF)
    row = lax.broadcasted_iota(jnp.int32, (8, TB), 0)

    def step(i, _):
        for t in range(8):
            block = i * 8 + t
            lanes = pl.ds(pl.multiple_of(block * TB, TB), TB)
            u, v = coord_ref[0:1, lanes], coord_ref[1:2, lanes]
            s = var_ref[pl.ds(block, 1), :]
            q = -HALF_LOG2E * (u * u + v * v)
            tile = jnp.where(row == 3, q, jnp.where(row == 4, s, jnp.where(row == 2, 1.0, 0.0)))
            tile = jnp.where(row == 0, u, jnp.where(row == 1, v, tile))
            h, m, l = split3(tile)
            stack = jnp.concatenate([h, h, m, m, h, l], axis=0).astype(BF)
            turned = lax.dot_general(eye, stack, (((1,), (1,)), ((), ())), preferred_element_type=F32)
            at_ref[lanes, :] = turned.astype(BF)
        return 0

    lax.fori_loop(0, blocks // 8, step, 0)


def match_items(codes_ref, first, count, spacing, at_ref, b_ref, acc_ref):
    row = lax.broadcasted_iota(jnp.int32, (8, TB), 0)

    def step(i, _):
        sums = []
        for t in range(UNROLL):
            code = codes_ref[first + i * UNROLL + t]
            block, start = code >> 16, code & 0xFFFF
            x = b_ref[pl.ds(start, 8, stride=spacing), :]
            u, v, s, p = x[0:1], x[1:2], x[VAR : VAR + 1], x[PRIOR : PRIOR + 1]
            q = -HALF_LOG2E * (u * u + v * v)
            near = jnp.where(row == 2, q, jnp.where(row == 3, 1.0, 0.0))
            near = jnp.where(row < 2, x * (2 * HALF_LOG2E), near)
            spread = jnp.where(row == 2, s, jnp.where(row == 4, 1.0, 0.0))
            h, m, l = split3(jnp.concatenate([near, spread], axis=1))
            stack = jnp.concatenate([h, m, h, m, l, h], axis=0).astype(BF)
            held = jnp.minimum(block, at_ref.shape[0] // TB - 1)
            a = at_ref[pl.ds(pl.multiple_of(held * TB, TB), TB), :]
            both = jnp.dot(a, stack, preferred_element_type=F32)
            r = 1.0 / both[:, TB:]
            w = r * jnp.exp2(both[:, :TB] * r)
            w_high = w.astype(BF)
            w_low = (w - w_high.astype(F32)).astype(BF)
            f = jnp.where(row == VAR, 1.0, x) * (2.0 * p)
            f_high = f.astype(BF).astype(F32)
            f_low = f - f_high
            left = jnp.concatenate(
                [
                    jnp.concatenate([f_high, f_high], axis=1),
                    jnp.concatenate([f_low, jnp.zeros_like(f_low)], axis=1),
                ],
                axis=0,
            ).astype(BF)
            right = jnp.concatenate([w_high, w_low], axis=1)
            o = lax.dot_general(left, right, (((1,), (1,)), ((), ())), preferred_element_type=F32)
            sums.append((block, o[0:8] + o[8:16]))
        for block, o in sums:
            acc_ref[block] += o
        return 0

    lax.fori_loop(0, lax.div(count + (UNROLL - 1), jnp.int32(UNROLL)), step, 0)


def match_kernel(blocks, length, spacing, parts, codes_ref, count_ref, at_ref, *refs):
    chunks, (out_ref, prob_ref, b_ref, acc_ref, sems) = refs[: -5], refs[-5:]
    phases = len(chunks) // parts
    rows = chunks[0].shape[0]
    copies = [
        pltpu.make_async_copy(
            chunk, b_ref.at[i // parts, pl.ds((i % parts) * rows, rows), :], sems.at[i]
        )
        for i, chunk in enumerate(chunks)
    ]
    for copy in copies:
        copy.start()
    acc_ref[...] = jnp.zeros_like(acc_ref)
    for p in range(phases):
        b_ref[p, pl.ds(parts * rows, b_ref.shape[1] - parts * rows), :] = jnp.zeros(
            (b_ref.shape[1] - parts * rows, TB), F32
        )
    for copy in copies:
        copy.wait()
    for p in range(phases):
        match_items(codes_ref, p * length, count_ref[p], spacing, at_ref, b_ref.at[p], acc_ref)

    def finish(i, _):
        for t in range(8):
            block = i * 8 + t
            a = acc_ref[block]
            s = a[5:6]
            inverse = 1.0 / (1.0 + s)
            out_ref[:, pl.ds(pl.multiple_of(block * TB, TB), TB)] = (a * inverse)[0:5]
            prob_ref[pl.ds(block, 1), :] = s * inverse
        return 0

    lax.fori_loop(0, blocks // 8, finish, 0)


def body(a_coord, a_var, dest, cand, cand_count, b_coord, b_var, b_prior, b_flux):
    zones, tiles = lax.axis_size("zone"), lax.axis_size("tile")
    blocks = dest.shape[0]
    slots = cand.shape[1]
    own_blocks = b_var.shape[0] // TB
    rows = NQ * own_blocks
    fast = is_grid({"zone": zones, "tile": tiles})
    grid = Grid(zones, tiles)

    shift = (cand >= MB).astype(jnp.int32) + (cand >= MB + own_blocks).astype(jnp.int32) - 1
    zone = dest // tiles + shift
    tile = dest % tiles
    block = cand - MB - shift * own_blocks
    live = (jnp.arange(slots, dtype=jnp.int32)[None, :] < cand_count) & (zone >= 0) & (zone < zones)
    if fast:
        phases = grid.high
        phase, row = locate(zone, tile, block, grid, rows)
    else:
        phases = 1
        phase, row = jnp.zeros_like(zone), (zone * tiles + tile) * rows + block
    here = jnp.arange(blocks, dtype=jnp.int32)[:, None]
    entry = jnp.where(live, (phase << 26) | (here << 16) | row, phases << 26)
    items = blocks * slots
    length = items + UNROLL
    codes, counts = pl.pallas_call(
        functools.partial(plan_kernel, items, phases, length, blocks << 16),
        out_shape=(
            jax.ShapeDtypeStruct(((phases + 1) * length,), jnp.int32),
            jax.ShapeDtypeStruct((8,), jnp.int32),
        ),
        in_specs=[SMEM],
        out_specs=(SMEM, SMEM),
        name="plan",
    )(entry.T.reshape(-1))

    var_rows = a_var.reshape(blocks, TB)
    at = pl.pallas_call(
        functools.partial(prep_kernel, blocks),
        out_shape=jax.ShapeDtypeStruct((blocks * TB, 48), BF),
        in_specs=[VMEM, VMEM],
        out_specs=VMEM,
        name="prep",
    )(a_coord, var_rows)

    own = jnp.concatenate([b_coord, b_flux, b_var[None, :], b_prior[None, :]], axis=0).reshape(rows, TB)
    if fast:
        chunks = [c for pair in gather_phases(own, grid) for c in pair]
        parts = 2
    else:
        chunks = [lax.all_gather(own, AXES, axis=0, tiled=True)]
        parts = 1
    buffer_rows = parts * chunks[0].shape[0] + own_blocks
    matched, prob = pl.pallas_call(
        functools.partial(match_kernel, blocks, length, own_blocks, parts),
        out_shape=(
            jax.ShapeDtypeStruct((5, blocks * TB), F32),
            jax.ShapeDtypeStruct((blocks, TB), F32),
        ),
        in_specs=[SMEM, SMEM, VMEM] + [ANY] * len(chunks),
        out_specs=(VMEM, VMEM),
        scratch_shapes=[
            pltpu.VMEM((len(chunks) // parts, buffer_rows, TB), F32),
            pltpu.VMEM((blocks + 1, 8, TB), F32),
            pltpu.SemaphoreType.DMA((len(chunks),)),
        ],
        name="match",
    )(codes, counts, at, *chunks)
    return matched, prob.reshape(-1)


def solution(mesh):
    placed = (
        P(None, AXES),
        P(AXES),
        P(AXES, None),
        P(AXES, None),
        P(AXES, None),
        P(None, AXES),
        P(AXES),
        P(AXES),
        P(None, AXES),
    )
    return jax.shard_map(
        body, mesh=mesh, in_specs=placed, out_specs=(P(None, AXES), P(AXES)), check_vma=False
    )
```

time: 608 us -> 117 us (0.19)
  matrix products: 371 us -> 0 us
  other arithmetic: 127 us -> 1.28 us
  Pallas kernels: 0 us -> 67.2 us
  local copies, waits for them, and re-layouts: 33.3 us -> 3.18 us
  waiting for transfers between devices: 51.7 us -> 26.9 us
    dot_general x16 -> x0, matrix products: 371 us -> none  [slot_match(): jnp.einsum('fj,ij->fi', block_data[:5], weight, precision=lax.Precision.H...]
    reduce_sum x5 -> x0, other arithmetic: 114 us -> none  [the longest x4 113 us: slot_match(): weight_sum = weight_sum + jnp.sum(weight, axis=1)]
    pallas_call x0 -> x3, Pallas kernels: none -> 67.2 us  [the longest x1 42.8 us: body(): pl.pallas_call(functools.partial(match_kernel, blocks, length, own_blocks...]
    all_to_all x3 -> x0, waiting for transfers between devices: 48.2 us -> none  [the longest x1 36.4 us: body(): lax.all_to_all(results, ('zone', 'tile'), split_axis=0, concat_axis=0, ti...]
    ppermute x2 -> x15, waiting for transfers between devices: 3.53 us -> 26.9 us  [the longest x4 19.7 us: gather_phases(): lax.ppermute(held, AXES, grid.side(True))]
    all_to_all x3 -> x0, starting transfers between devices: 17 us -> none  [the longest x1 7.08 us: body(): lax.all_to_all(send_labels.reshape(devices, capacity, K + 1), ('zone', 't...]
    gather x17 -> x0, local copies, waits for them, and re-layouts: 15.5 us -> none  [the longest x16 13.2 us: match_one(): candidates.append(window[block_index])]
    ppermute x2 -> x15, starting transfers between devices: 4.55 us -> 17.4 us  [the longest x4 7.12 us: gather_phases(): phases.append((four, lax.ppermute(four, AXES, grid.core())))]
  transfers between devices with their start and end apart: 5 -> 15, of which waited for: 4 -> 6; matrix products, arithmetic and copies ran while one was open for 2% -> 3% of each run, Pallas kernels for 0% -> 21%
where the time goes in v1:
time: 117 us
  Pallas kernels  67.2 us (57%)
  waiting for transfers between devices  26.9 us (23%)
  starting transfers between devices  17.4 us (15%)
  local copies, waits for them, and re-layouts  3.18 us (3%)
  other arithmetic  1.28 us (1%)
    pallas_call x1, Pallas kernels, body(): pl.pallas_call(functools.partial(match_kernel, blocks, length, own_blocks...  42.8 us
    ppermute x4, waiting for transfers between devices, gather_phases(): lax.ppermute(held, AXES, grid.side(True))  19.7 us
    pallas_call x1, Pallas kernels, body(): pl.pallas_call(functools.partial(plan_kernel, items, phases, length, bloc...  13.1 us
    pallas_call x1, Pallas kernels, body(): pl.pallas_call(functools.partial(prep_kernel, blocks), out_shape=jax.Shap...  11.4 us
    ppermute x4, starting transfers between devices, gather_phases(): phases.append((four, lax.ppermute(four, AXES, grid.core())))  7.12 us
    ppermute x4, starting transfers between devices, gather_phases(): lax.ppermute(pair, AXES, grid.side(False))  4.61 us
    ppermute x4, waiting for transfers between devices, gather_phases(): lax.ppermute(pair, AXES, grid.side(False))  4.28 us
    ppermute x4, starting transfers between devices, gather_phases(): lax.ppermute(held, AXES, grid.side(True))  3.07 us
  transfers between devices with their start and end apart: 15, of which 6 were waited for; matrix products, arithmetic and copies ran while one was open for 3% of the time, Pallas kernels for 21%

profile of v1, /device:TPU:1, one launch (start us, length us, event | category | flops | bytes accessed | tf_op | source)
XLA Modules:
  0.0 116.8 jit_solution(14395884493292781950)
XLA Ops:
  0.7 1.1 pad_maximum_fusion.4
  1.8 0.1 reshape.23
  1.9 2.1 %collective-permute-start = (f32[448,128]{1,0:T(8,128)S(1)}, f32[448,128]{1,0:T(8,128)S(1)}, u32[]{:S(2)}, u32[]{:S(2)}) collective-permute-start(f32[448,128]{1,0:T(8,128)S(1)} %reshape.23), channel_id=1, source_target_pairs={{0,4},{1,3},{2,6},{3,1},{4,0},{5,7},{6,2},{7,5},{8,12},{9,11},{10,... | collective-permute-start | bytes 688136 | tf_op jit(solution)/shard_map/ppermute | solution.py:61
  4.0 1.3 %collective-permute-start.3 = (f32[448,128]{1,0:T(8,128)S(1)}, f32[448,128]{1,0:T(8,128)S(1)}, u32[]{:S(2)}, u32[]{:S(2)}) collective-permute-start(f32[448,128]{1,0:T(8,128)S(1)} %reshape.23), channel_id=1, source_target_pairs={{0,8},{1,9},{2,10},{3,11},{4,12},{5,13},{6,14},{7,15},{8,16},{9,17... | collective-permute-start | bytes 688136 | tf_op jit(solution)/shard_map/ppermute | solution.py:60
  5.3 0.7 constant_dynamic-update-slice_fusion.2
  6.0 1.7 %collective-permute-done = f32[448,128]{1,0:T(8,128)S(1)} collective-permute-done((f32[448,128]{1,0:T(8,128)S(1)}, f32[448,128]{1,0:T(8,128)S(1)}, u32[]{:S(2)}, u32[]{:S(2)}) %collective-permute-start) | collective-permute-done | bytes 229408 | tf_op jit(solution)/shard_map/ppermute | solution.py:61
  7.7 1.5 %collective-permute-start.1 = (f32[896,128]{1,0:T(8,128)S(1)}, f32[896,128]{1,0:T(8,128)S(1)}, u32[]{:S(2)}, u32[]{:S(2)}) collective-permute-start(f32[896,128]{1,0:T(8,128)S(1)} %pad_maximum_fusion), channel_id=1, source_target_pairs={{0,2},{1,5},{2,0},{3,7},{4,6},{5,1},{6,4},{7,3},{8,10},{9,13},{10,... | collective-permute-start | bytes 1376264 | tf_op jit(solution)/shard_map/ppermute | solution.py:62
  9.2 2.9 %collective-permute-done.3 = f32[448,128]{1,0:T(8,128)S(1)} collective-permute-done((f32[448,128]{1,0:T(8,128)S(1)}, f32[448,128]{1,0:T(8,128)S(1)}, u32[]{:S(2)}, u32[]{:S(2)}) %collective-permute-start.3) | collective-permute-done | bytes 229408 | tf_op jit(solution)/shard_map/ppermute | solution.py:60
  12.2 0.0 collective-permute-start.7
  12.2 0.0 collective-permute-start.4
  12.2 0.7 constant_dynamic-update-slice_fusion.1
  12.9 6.7 %collective-permute-done.4 = f32[448,128]{1,0:T(8,128)S(1)} collective-permute-done((f32[448,128]{1,0:T(8,128)S(1)}, f32[448,128]{1,0:T(8,128)S(1)}, u32[]{:S(2)}, u32[]{:S(2)}) %collective-permute-start.4) | collective-permute-done | bytes 229408 | tf_op jit(solution)/shard_map/ppermute | solution.py:61
  19.6 1.8 %collective-permute-start.5 = (f32[896,128]{1,0:T(8,128)S(1)}, f32[896,128]{1,0:T(8,128)S(1)}, u32[]{:S(2)}, u32[]{:S(2)}) collective-permute-start(f32[896,128]{1,0:T(8,128)S(1)} %pad_maximum_fusion.1), channel_id=1, source_target_pairs={{0,2},{1,5},{2,0},{3,7},{4,6},{5,1},{6,4},{7,3},{8,10},{9,13},{10,... | collective-permute-start | bytes 1376264 | tf_op jit(solution)/shard_map/ppermute | solution.py:62
  21.4 1.3 %collective-permute-start.11 = (f32[448,128]{1,0:T(8,128)S(1)}, f32[448,128]{1,0:T(8,128)S(1)}, u32[]{:S(2)}, u32[]{:S(2)}) collective-permute-start(f32[448,128]{1,0:T(8,128)S(1)} %collective-permute-done.7), channel_id=1, source_target_pairs={{0,8},{1,9},{2,10},{3,11},{4,12},{5,13},{6,14},{7,15},{8,16},{9,17... | collective-permute-start | bytes 688136 | tf_op jit(solution)/shard_map/ppermute | solution.py:60
  22.7 0.0 collective-permute-start.8
  22.8 7.5 %collective-permute-done.8 = f32[448,128]{1,0:T(8,128)S(1)} collective-permute-done((f32[448,128]{1,0:T(8,128)S(1)}, f32[448,128]{1,0:T(8,128)S(1)}, u32[]{:S(2)}, u32[]{:S(2)}) %collective-permute-start.8) | collective-permute-done | bytes 229408 | tf_op jit(solution)/shard_map/ppermute | solution.py:61
  30.4 0.3 collective-permute-start.9
  30.7 0.9 collective-permute-start.12
  31.6 0.8 constant_dynamic-update-slice_fusion.refs_0_
  32.4 1.8 %collective-permute-start.2 = (f32[1792,128]{1,0:T(8,128)}, f32[1792,128]{1,0:T(8,128)}, u32[]{:S(2)}, u32[]{:S(2)}) collective-permute-start(f32[1792,128]{1,0:T(8,128)} %constant_dynamic-update-slice_fusion.refs_0_), channel_id=1, source_target_pairs={{0,1},{1,0},{2,3},{3,2},{4,5},{5,4},{6,7},{7,6},{8,9},{9,8},{10,11... | collective-permute-start | bytes 2752520 | tf_op jit(solution)/shard_map/ppermute | solution.py:63
  34.2 3.8 %collective-permute-done.12 = f32[448,128]{1,0:T(8,128)S(1)} collective-permute-done((f32[448,128]{1,0:T(8,128)S(1)}, f32[448,128]{1,0:T(8,128)S(1)}, u32[]{:S(2)}, u32[]{:S(2)}) %collective-permute-start.12) | collective-permute-done | bytes 229408 | tf_op jit(solution)/shard_map/ppermute | solution.py:61
  38.0 1.0 collective-permute-start.13
  39.1 2.2 %collective-permute-start.6 = (f32[1792,128]{1,0:T(8,128)S(1)}, f32[1792,128]{1,0:T(8,128)}, u32[]{:S(2)}, u32[]{:S(2)}) collective-permute-start(f32[1792,128]{1,0:T(8,128)S(1)} %constant_dynamic-update-slice_fusion.3.refs_2_), channel_id=1, source_target_pairs={{0,1},{1,0},{2,3},{3,2},{4,5},{5,4},{6,7},{7,6},{8,9},{9,8},{10,11... | collective-permute-start | bytes 2752520 | tf_op jit(solution)/shard_map/ppermute | solution.py:63
  41.3 0.0 collective-permute-done.9
  41.4 0.1 collective-permute-start.10
  41.5 4.3 %collective-permute-done.13 = f32[896,128]{1,0:T(8,128)S(1)} collective-permute-done((f32[896,128]{1,0:T(8,128)S(1)}, f32[896,128]{1,0:T(8,128)S(1)}, u32[]{:S(2)}, u32[]{:S(2)}) %collective-permute-start.13) | collective-permute-done | bytes 458784 | tf_op jit(solution)/shard_map/ppermute | solution.py:62
  45.8 3.1 %collective-permute-start.14 = (f32[1792,128]{1,0:T(8,128)S(1)}, f32[1792,128]{1,0:T(8,128)}, u32[]{:S(2)}, u32[]{:S(2)}) collective-permute-start(f32[1792,128]{1,0:T(8,128)S(1)} %constant_dynamic-update-slice_fusion.9.refs_6_), channel_id=1, source_target_pairs={{0,1},{1,0},{2,3},{3,2},{4,5},{5,4},{6,7},{7,6},{8,9},{9,8},{10,11... | collective-permute-start | bytes 2752520 | tf_op jit(solution)/shard_map/ppermute | solution.py:63
  48.9 0.6 copy.11
  49.5 13.1 %plan.1 = (s32[5200]{0:T(1024)}, s32[8]{0:T(128)}) custom-call(s32[1024]{0:T(1024)} %bitcast.16), custom_call_target="tpu_custom_call" | custom-call | tf_op jit(solution)/shard_map/plan/pallas_call | solution.py:225
  62.6 11.4 %prep.1.at_ref = bf16[32768,48]{1,0:T(8,128)(2,1)} custom-call(f32[2,32768]{1,0:T(2,128)} %coord_ref.1, f32[256,128]{1,0:T(8,128)} %bitcast.13), custom_call_target="tpu_custom_call" | custom-call | tf_op jit(solution)/shard_map/prep/pallas_call | solution.py:237
  74.0 0.0 collective-permute-done.14.refs_7_
  74.0 42.8 %match.1 = (f32[5,32768]{1,0:T(8,128)}, f32[256,128]{1,0:T(8,128)}) custom-call(s32[5200]{0:T(1024)} %get-tuple-element.6.codes_ref, s32[8]{0:T(128)} %get-tuple-element.7.count_ref, bf16[32768,48]{1,0:T(8,128)(2,1)} %prep.1.at_ref, f32[1792,128]{1,0:T(8,128)} %constant_dynamic-update-slice_fusion.refs_0_, f32[1792,128]{1,0:T(8,128)} %collective-permute-done.2.refs_1_, ...), custom_call_target="tpu_custom_call" | custom-call | tf_op jit(solution)/shard_map/match/pallas_call | solution.py:253
  (36 shorter events, 0.4 us)
Async XLA Ops:
  0.6 48.2 %copy-start.4 = (s32[256,1]{0,1:T(1,128)S(1)}, s32[256,1]{0,1:T(1,128)}, u32[]{:S(2)}) copy-start(s32[256,1]{0,1:T(1,128)} %param.11) | copy-start | bytes 3076
  0.6 48.3 %copy-start.5 = (s32[256,1]{0,1:T(1,128)S(1)}, s32[256,1]{0,1:T(1,128)}, u32[]{:S(2)}) copy-start(s32[256,1]{0,1:T(1,128)} %param.13) | copy-start | bytes 3076
  0.7 48.3 %copy-start.3 = (s32[256,4]{0,1:T(4,128)S(1)}, s32[256,4]{0,1:T(4,128)}, u32[]{:S(2)}) copy-start(s32[256,4]{0,1:T(4,128)} %param.12) | copy-start | bytes 12292
  1.9 5.8 %collective-permute-start = (f32[448,128]{1,0:T(8,128)S(1)}, f32[448,128]{1,0:T(8,128)S(1)}, u32[]{:S(2)}, u32[]{:S(2)}) collective-permute-start(f32[448,128]{1,0:T(8,128)S(1)} %reshape.23), channel_id=1, source_target_pairs={{0,4},{1,3},{2,6},{3,1},{4,0},{5,7},{6,2},{7,5},{8,12},{9,11},{10,... | collective-permute-start | bytes 688136 | tf_op jit(solution)/shard_map/ppermute | solution.py:61
  4.0 8.2 %collective-permute-start.3 = (f32[448,128]{1,0:T(8,128)S(1)}, f32[448,128]{1,0:T(8,128)S(1)}, u32[]{:S(2)}, u32[]{:S(2)}) collective-permute-start(f32[448,128]{1,0:T(8,128)S(1)} %reshape.23), channel_id=1, source_target_pairs={{0,8},{1,9},{2,10},{3,11},{4,12},{5,13},{6,14},{7,15},{8,16},{9,17... | collective-permute-start | bytes 688136 | tf_op jit(solution)/shard_map/ppermute | solution.py:60
  7.7 23.9 %collective-permute-start.1 = (f32[896,128]{1,0:T(8,128)S(1)}, f32[896,128]{1,0:T(8,128)S(1)}, u32[]{:S(2)}, u32[]{:S(2)}) collective-permute-start(f32[896,128]{1,0:T(8,128)S(1)} %pad_maximum_fusion), channel_id=1, source_target_pairs={{0,2},{1,5},{2,0},{3,7},{4,6},{5,1},{6,4},{7,3},{8,10},{9,13},{10,... | collective-permute-start | bytes 1376264 | tf_op jit(solution)/shard_map/ppermute | solution.py:62
  12.2 9.3 %collective-permute-start.7 = (f32[448,128]{1,0:T(8,128)S(1)}, f32[448,128]{1,0:T(8,128)S(1)}, u32[]{:S(2)}, u32[]{:S(2)}) collective-permute-start(f32[448,128]{1,0:T(8,128)S(1)} %collective-permute-done.3), channel_id=1, source_target_pairs={{0,8},{1,9},{2,10},{3,11},{4,12},{5,13},{6,14},{7,15},{8,16},{9,17... | collective-permute-start | bytes 688136 | tf_op jit(solution)/shard_map/ppermute | solution.py:60
  12.2 7.4 %collective-permute-start.4 = (f32[448,128]{1,0:T(8,128)S(1)}, f32[448,128]{1,0:T(8,128)S(1)}, u32[]{:S(2)}, u32[]{:S(2)}) collective-permute-start(f32[448,128]{1,0:T(8,128)S(1)} %collective-permute-done.3), channel_id=1, source_target_pairs={{0,4},{1,3},{2,6},{3,1},{4,0},{5,7},{6,2},{7,5},{8,12},{9,11},{10,... | collective-permute-start | bytes 688136 | tf_op jit(solution)/shard_map/ppermute | solution.py:61
  19.6 19.4 %collective-permute-start.5 = (f32[896,128]{1,0:T(8,128)S(1)}, f32[896,128]{1,0:T(8,128)S(1)}, u32[]{:S(2)}, u32[]{:S(2)}) collective-permute-start(f32[896,128]{1,0:T(8,128)S(1)} %pad_maximum_fusion.1), channel_id=1, source_target_pairs={{0,2},{1,5},{2,0},{3,7},{4,6},{5,1},{6,4},{7,3},{8,10},{9,13},{10,... | collective-permute-start | bytes 1376264 | tf_op jit(solution)/shard_map/ppermute | solution.py:62
  21.4 9.3 %collective-permute-start.11 = (f32[448,128]{1,0:T(8,128)S(1)}, f32[448,128]{1,0:T(8,128)S(1)}, u32[]{:S(2)}, u32[]{:S(2)}) collective-permute-start(f32[448,128]{1,0:T(8,128)S(1)} %collective-permute-done.7), channel_id=1, source_target_pairs={{0,8},{1,9},{2,10},{3,11},{4,12},{5,13},{6,14},{7,15},{8,16},{9,17... | collective-permute-start | bytes 688136 | tf_op jit(solution)/shard_map/ppermute | solution.py:60
  22.7 7.6 %collective-permute-start.8 = (f32[448,128]{1,0:T(8,128)S(1)}, f32[448,128]{1,0:T(8,128)S(1)}, u32[]{:S(2)}, u32[]{:S(2)}) collective-permute-start(f32[448,128]{1,0:T(8,128)S(1)} %collective-permute-done.7), channel_id=1, source_target_pairs={{0,4},{1,3},{2,6},{3,1},{4,0},{5,7},{6,2},{7,5},{8,12},{9,11},{10,... | collective-permute-start | bytes 688136 | tf_op jit(solution)/shard_map/ppermute | solution.py:61
  30.4 11.0 %collective-permute-start.9 = (f32[896,128]{1,0:T(8,128)S(1)}, f32[896,128]{1,0:T(8,128)S(1)}, u32[]{:S(2)}, u32[]{:S(2)}) collective-permute-start(f32[896,128]{1,0:T(8,128)S(1)} %pad_maximum_fusion.2), channel_id=1, source_target_pairs={{0,2},{1,5},{2,0},{3,7},{4,6},{5,1},{6,4},{7,3},{8,10},{9,13},{10,... | collective-permute-start | bytes 1376264 | tf_op jit(solution)/shard_map/ppermute | solution.py:62
  30.7 7.3 %collective-permute-start.12 = (f32[448,128]{1,0:T(8,128)S(1)}, f32[448,128]{1,0:T(8,128)S(1)}, u32[]{:S(2)}, u32[]{:S(2)}) collective-permute-start(f32[448,128]{1,0:T(8,128)S(1)} %collective-permute-done.11), channel_id=1, source_target_pairs={{0,4},{1,3},{2,6},{3,1},{4,0},{5,7},{6,2},{7,5},{8,12},{9,11},{10,... | collective-permute-start | bytes 688136 | tf_op jit(solution)/shard_map/ppermute | solution.py:61
  32.4 41.6 %collective-permute-start.2 = (f32[1792,128]{1,0:T(8,128)}, f32[1792,128]{1,0:T(8,128)}, u32[]{:S(2)}, u32[]{:S(2)}) collective-permute-start(f32[1792,128]{1,0:T(8,128)} %constant_dynamic-update-slice_fusion.refs_0_), channel_id=1, source_target_pairs={{0,1},{1,0},{2,3},{3,2},{4,5},{5,4},{6,7},{7,6},{8,9},{9,8},{10,11... | collective-permute-start | bytes 2752520 | tf_op jit(solution)/shard_map/ppermute | solution.py:63
  38.0 7.7 %collective-permute-start.13 = (f32[896,128]{1,0:T(8,128)S(1)}, f32[896,128]{1,0:T(8,128)S(1)}, u32[]{:S(2)}, u32[]{:S(2)}) collective-permute-start(f32[896,128]{1,0:T(8,128)S(1)} %pad_maximum_fusion.3), channel_id=1, source_target_pairs={{0,2},{1,5},{2,0},{3,7},{4,6},{5,1},{6,4},{7,3},{8,10},{9,13},{10,... | collective-permute-start | bytes 1376264 | tf_op jit(solution)/shard_map/ppermute | solution.py:62
  39.1 34.9 %copy-start.1 = (f32[1792,128]{1,0:T(8,128)}, f32[1792,128]{1,0:T(8,128)S(1)}, u32[]{:S(2)}) copy-start(f32[1792,128]{1,0:T(8,128)S(1)} %constant_dynamic-update-slice_fusion.3.refs_2_) | copy-start | bytes 2752516
  39.1 34.9 %collective-permute-start.6 = (f32[1792,128]{1,0:T(8,128)S(1)}, f32[1792,128]{1,0:T(8,128)}, u32[]{:S(2)}, u32[]{:S(2)}) collective-permute-start(f32[1792,128]{1,0:T(8,128)S(1)} %constant_dynamic-update-slice_fusion.3.refs_2_), channel_id=1, source_target_pairs={{0,1},{1,0},{2,3},{3,2},{4,5},{5,4},{6,7},{7,6},{8,9},{9,8},{10,11... | collective-permute-start | bytes 2752520 | tf_op jit(solution)/shard_map/ppermute | solution.py:63
  41.4 32.7 %copy-start = (f32[1792,128]{1,0:T(8,128)}, f32[1792,128]{1,0:T(8,128)S(1)}, u32[]{:S(2)}) copy-start(f32[1792,128]{1,0:T(8,128)S(1)} %constant_dynamic-update-slice_fusion.6.refs_4_) | copy-start | bytes 2752516
  41.4 32.6 %collective-permute-start.10 = (f32[1792,128]{1,0:T(8,128)S(1)}, f32[1792,128]{1,0:T(8,128)}, u32[]{:S(2)}, u32[]{:S(2)}) collective-permute-start(f32[1792,128]{1,0:T(8,128)S(1)} %constant_dynamic-update-slice_fusion.6.refs_4_), channel_id=1, source_target_pairs={{0,1},{1,0},{2,3},{3,2},{4,5},{5,4},{6,7},{7,6},{8,9},{9,8},{10,11... | collective-permute-start | bytes 2752520 | tf_op jit(solution)/shard_map/ppermute | solution.py:63
  45.8 28.3 %copy-start.2 = (f32[1792,128]{1,0:T(8,128)}, f32[1792,128]{1,0:T(8,128)S(1)}, u32[]{:S(2)}) copy-start(f32[1792,128]{1,0:T(8,128)S(1)} %constant_dynamic-update-slice_fusion.9.refs_6_) | copy-start | bytes 2752516
  45.8 28.2 %collective-permute-start.14 = (f32[1792,128]{1,0:T(8,128)S(1)}, f32[1792,128]{1,0:T(8,128)}, u32[]{:S(2)}, u32[]{:S(2)}) collective-permute-start(f32[1792,128]{1,0:T(8,128)S(1)} %constant_dynamic-update-slice_fusion.9.refs_6_), channel_id=1, source_target_pairs={{0,1},{1,0},{2,3},{3,2},{4,5},{5,4},{6,7},{7,6},{8,9},{9,8},{10,11... | collective-permute-start | bytes 2752520 | tf_op jit(solution)/shard_map/ppermute | solution.py:63

commit v2 on v1

v2 whole, which is shorter than its diff:
```python
import functools
import math

import jax
import jax.numpy as jnp
from jax import lax
from jax.experimental import pallas as pl
from jax.experimental.pallas import tpu as pltpu
from jax.sharding import PartitionSpec as P


TB = 128
MB = 8
NQ = 7
VAR, PRIOR = 5, 6
UNROLL = 32
BF, F32 = jnp.bfloat16, jnp.float32
HALF_LOG2E = 0.5 * math.log2(math.e)
AXES = ("zone", "tile")
VMEM = pl.BlockSpec(memory_space=pltpu.VMEM)
SMEM = pl.BlockSpec(memory_space=pltpu.SMEM)


def params(mib):
    return pltpu.CompilerParams(vmem_limit_bytes=mib << 20)


def split3(x):
    high = x.astype(BF).astype(F32)
    middle = (x - high).astype(BF).astype(F32)
    return high, middle, x - high - middle


def is_grid(mesh_shape):
    return mesh_shape["zone"] % 2 == 0 and mesh_shape["tile"] == 4


class Grid:
    def __init__(self, zones, tiles):
        self.zones, self.tiles, self.high = zones, tiles, zones // 2

    def perm(self, move):
        pairs = []
        for d in range(self.zones * self.tiles):
            zone, tile = divmod(d, self.tiles)
            h, x, y, c = move(zone // 2, zone % 2, tile // 2, tile % 2)
            pairs.append((d, ((h % self.high) * 2 + x) * self.tiles + y * 2 + c))
        return pairs

    def shift(self, by):
        return self.perm(lambda h, x, y, c: (h + by, x, y, c))

    def side(self, first):
        return self.perm(lambda h, x, y, c: (h, x ^ 1, y, c) if (c == 0) == first else (h, x, y ^ 1, c))

    def core(self):
        return self.perm(lambda h, x, y, c: (h, x, y, c ^ 1))


def send(array, pairs):
    return lax.ppermute(array, AXES, pairs)


def gather_phases(own, grid):
    n = grid.high
    held = {0: own}
    order = [0]
    for step in range(1, n // 2 + 1):
        for s, back in ((step, 1), (n - step, -1)):
            if s not in held:
                held[s] = send(held[(s - back) % n], grid.shift(back))
                order.append(s)
    phases = []
    for s in order:
        z = held[s]
        pair = jnp.concatenate([z, send(z, grid.side(True))], axis=0)
        four = jnp.concatenate([pair, send(pair, grid.side(False))], axis=0)
        phases.append((four, send(four, grid.core())))
    return phases, order


def locate(zone, tile, block, grid, rows):
    my_zone, my_tile = lax.axis_index("zone"), lax.axis_index("tile")
    distance = lax.rem((my_zone >> 1) - (zone >> 1) + grid.high, grid.high)
    dx = (zone & 1) ^ (my_zone & 1)
    dy = ((tile >> 1) ^ (my_tile >> 1)) & 1
    dc = (tile ^ my_tile) & 1
    place = jnp.where((tile & 1) == 0, dx + 2 * dy, dy + 2 * dx)
    return distance, (dc << 16) | (place * rows + block)


def plan_kernel(phases, length, dummy, entry_ref, codes_ref, count_ref, place_ref, work_ref, sem):
    entry = entry_ref[...]
    high = entry.shape[0]
    phase = entry >> 27
    lanes = (TB, TB)
    earlier = lax.broadcasted_iota(jnp.int32, lanes, 0) < lax.broadcasted_iota(jnp.int32, lanes, 1)
    sums = jnp.concatenate([jnp.where(earlier, 1.0, 0.0), jnp.ones(lanes, F32)], axis=1).astype(BF)
    above = lax.broadcasted_iota(jnp.int32, (high, high), 1) < lax.broadcasted_iota(jnp.int32, (high, high), 0)
    above = jnp.where(above, 1.0, 0.0).astype(BF)
    place = phase * length
    totals = []
    for p in range(phases + 1):
        member = jnp.where(phase == p, 1.0, 0.0)
        both = jnp.dot(member.astype(BF), sums, preferred_element_type=F32)
        before, total = both[:, :TB], both[:, TB:]
        rows = jnp.dot(above, total.astype(BF), preferred_element_type=F32)
        place = place + jnp.where(phase == p, (before + rows).astype(jnp.int32), 0)
        totals.append(jnp.sum(total, axis=0, keepdims=True).astype(jnp.int32))
    place_ref[pl.ds(0, high), :] = place
    place_ref[pl.ds(high, high), :] = entry & ((1 << 27) - 1)
    place_ref[pl.ds(2 * high, 8), :] = jnp.concatenate(
        totals + [jnp.zeros((1, TB), jnp.int32)] * (7 - phases), axis=0
    )
    copy = pltpu.make_async_copy(place_ref, work_ref, sem)
    copy.start()
    copy.wait()

    def row(r, _):
        def step(i, _):
            for t in range(16):
                codes_ref[work_ref[r, i * 16 + t]] = work_ref[high + r, i * 16 + t]
            return 0

        return lax.fori_loop(0, TB // 16, step, 0)

    lax.fori_loop(0, high, row, 0)
    for p in range(phases):
        count = work_ref[2 * high + p, 0]
        for t in range(UNROLL):
            codes_ref[p * length + count + t] = jnp.int32(dummy)
        count_ref[p] = count


def prep_kernel(blocks, coord_ref, var_ref, at_ref):
    eye = jnp.where(
        lax.broadcasted_iota(jnp.int32, (TB, TB), 0) == lax.broadcasted_iota(jnp.int32, (TB, TB), 1), 1.0, 0.0
    ).astype(BF)
    row = lax.broadcasted_iota(jnp.int32, (8, TB), 0)

    def step(i, _):
        for t in range(8):
            block = i * 8 + t
            lanes = pl.ds(pl.multiple_of(block * TB, TB), TB)
            u, v = coord_ref[0:1, lanes], coord_ref[1:2, lanes]
            s = var_ref[pl.ds(block, 1), :]
            q = -HALF_LOG2E * (u * u + v * v)
            tile = jnp.where(row == 3, q, jnp.where(row == 4, s, jnp.where(row == 2, 1.0, 0.0)))
            tile = jnp.where(row == 0, u, jnp.where(row == 1, v, tile))
            h, m, l = split3(tile)
            stack = jnp.concatenate([h, h, m, m, h, l], axis=0).astype(BF)
            turned = lax.dot_general(eye, stack, (((1,), (1,)), ((), ())), preferred_element_type=F32)
            at_ref[lanes, :] = turned.astype(BF)
        return 0

    lax.fori_loop(0, blocks // 8, step, 0)


def match_items(codes_ref, first, count, spacing, at_ref, b_refs, acc_ref):
    row = lax.broadcasted_iota(jnp.int32, (8, TB), 0)
    gap = jnp.zeros((8 - NQ, TB), F32)

    def step(i, _):
        sums = []
        for t in range(UNROLL):
            code = codes_ref[first + i * UNROLL + t]
            block, half, start = code >> 17, (code >> 16) & 1, code & 0xFFFF
            x = b_refs[0][pl.ds(start, NQ, stride=spacing), :]
            if len(b_refs) > 1:
                x = jnp.where(half == 1, b_refs[1][pl.ds(start, NQ, stride=spacing), :], x)
            x = jnp.concatenate([x, gap], axis=0)
            u, v, s, p = x[0:1], x[1:2], x[VAR : VAR + 1], x[PRIOR : PRIOR + 1]
            q = -HALF_LOG2E * (u * u + v * v)
            near = jnp.where(row == 2, q, jnp.where(row == 3, 1.0, 0.0))
            near = jnp.where(row < 2, x * (2 * HALF_LOG2E), near)
            spread = jnp.where(row == 2, s, jnp.where(row == 4, 1.0, 0.0))
            h, m, l = split3(jnp.concatenate([near, spread], axis=1))
            stack = jnp.concatenate([h, m, h, m, l, h], axis=0).astype(BF)
            held = jnp.minimum(block, at_ref.shape[0] // TB - 1)
            a = at_ref[pl.ds(pl.multiple_of(held * TB, TB), TB), :]
            both = jnp.dot(a, stack, preferred_element_type=F32)
            r = 1.0 / both[:, TB:]
            w = r * jnp.exp2(both[:, :TB] * r)
            w_high = w.astype(BF)
            w_low = (w - w_high.astype(F32)).astype(BF)
            f = jnp.where(row == VAR, 1.0, x) * (2.0 * p)
            f_high = f.astype(BF).astype(F32)
            f_low = f - f_high
            left = jnp.concatenate(
                [
                    jnp.concatenate([f_high, f_high], axis=1),
                    jnp.concatenate([f_low, jnp.zeros_like(f_low)], axis=1),
                ],
                axis=0,
            ).astype(BF)
            right = jnp.concatenate([w_high, w_low], axis=1)
            o = lax.dot_general(left, right, (((1,), (1,)), ((), ())), preferred_element_type=F32)
            sums.append((block, o[0:8] + o[8:16]))
        for block, o in sums:
            acc_ref[block] += o
        return 0

    lax.fori_loop(0, lax.div(count + (UNROLL - 1), jnp.int32(UNROLL)), step, 0)


def match_kernel(blocks, place, length, spacing, first, last, codes_ref, count_ref, at_ref, *refs):
    refs = list(refs)
    if last:
        out_ref, prob_ref, acc_ref = refs[-3:]
        refs = refs[:-3]
    else:
        acc_ref = refs.pop()
    if first:
        acc_ref[...] = jnp.zeros_like(acc_ref)
    elif last:
        acc_ref[...] = refs.pop()[...]
    else:
        refs.pop()
    match_items(codes_ref, place * length, count_ref[place], spacing, at_ref, refs, acc_ref)
    if not last:
        return

    def finish(i, _):
        for t in range(8):
            block = i * 8 + t
            a = acc_ref[block]
            s = a[5:6]
            inverse = 1.0 / (1.0 + s)
            out_ref[:, pl.ds(pl.multiple_of(block * TB, TB), TB)] = (a * inverse)[0:5]
            prob_ref[pl.ds(block, 1), :] = s * inverse
        return 0

    lax.fori_loop(0, blocks // 8, finish, 0)


def match(blocks, place, length, spacing, last, codes, counts, at, arrays, acc):
    sums = jax.ShapeDtypeStruct((blocks + 1, 8, TB), F32)
    outs = (jax.ShapeDtypeStruct((5, blocks * TB), F32), jax.ShapeDtypeStruct((blocks, TB), F32))
    args = [codes, counts, at, *arrays] + ([] if acc is None else [acc])
    return pl.pallas_call(
        functools.partial(match_kernel, blocks, place, length, spacing, acc is None, last),
        out_shape=outs if last else sums,
        in_specs=[SMEM, SMEM] + [VMEM] * (len(args) - 2),
        out_specs=(VMEM, VMEM) if last else VMEM,
        scratch_shapes=[pltpu.VMEM(sums.shape, F32)] if last else [],
        input_output_aliases={} if last or acc is None else {len(args) - 1: 0},
        compiler_params=params(12),
        cost_estimate=pl.CostEstimate(flops=4 * 10**9, transcendentals=5 * 10**6, bytes_accessed=10**7),
    )(*args)


def work(a_coord, a_var, dest, cand, cand_count, b_coord, b_var, b_prior, b_flux):
    zones, tiles = lax.axis_size("zone"), lax.axis_size("tile")
    blocks = dest.shape[0]
    slots = cand.shape[1]
    own_blocks = b_var.shape[0] // TB
    rows = NQ * own_blocks
    fast = is_grid({"zone": zones, "tile": tiles})
    grid = Grid(zones, tiles)

    shift = (cand >= MB).astype(jnp.int32) + (cand >= MB + own_blocks).astype(jnp.int32) - 1
    zone = dest // tiles + shift
    tile = dest % tiles
    block = cand - MB - shift * own_blocks
    live = (jnp.arange(slots, dtype=jnp.int32)[None, :] < cand_count) & (zone >= 0) & (zone < zones)
    own = jnp.concatenate([b_coord, b_flux, b_var[None, :], b_prior[None, :]], axis=0).reshape(rows, TB)
    if fast:
        arrays, order = gather_phases(own, grid)
        phase, code = locate(zone, tile, block, grid, rows)
    else:
        arrays, order = [(lax.all_gather(own, AXES, axis=0, tiled=True),)], [0]
        phase, code = jnp.zeros_like(zone), (zone * tiles + tile) * rows + block
    phases = len(order)
    here = jnp.arange(blocks, dtype=jnp.int32)[:, None]
    entry = jnp.where(live, (phase << 27) | (here << 17) | code, phases << 27)
    items = blocks * slots
    length = items + UNROLL
    plan = pl.pallas_call(
        functools.partial(plan_kernel, phases, length, blocks << 17),
        out_shape=(
            jax.ShapeDtypeStruct(((phases + 1) * length,), jnp.int32),
            jax.ShapeDtypeStruct((8,), jnp.int32),
        ),
        in_specs=[VMEM],
        out_specs=(SMEM, SMEM),
        scratch_shapes=[
            pltpu.VMEM((2 * items // TB + 8, TB), jnp.int32),
            pltpu.SMEM((2 * items // TB + 8, TB), jnp.int32),
            pltpu.SemaphoreType.DMA(()),
        ],
        compiler_params=params(4),
        cost_estimate=pl.CostEstimate(flops=10**9, transcendentals=0, bytes_accessed=10**6),
        name="plan",
    )
    codes, counts = plan(entry.T.reshape(items // TB, TB))

    var_rows = a_var.reshape(blocks, TB)
    prep = pl.pallas_call(
        functools.partial(prep_kernel, blocks),
        out_shape=jax.ShapeDtypeStruct((blocks * TB, 48), BF),
        in_specs=[VMEM, VMEM],
        out_specs=VMEM,
        compiler_params=params(4),
        cost_estimate=pl.CostEstimate(flops=4 * 10**9, transcendentals=0, bytes_accessed=10**7),
        name="prep",
    )
    at = prep(a_coord, var_rows)
    at = pltpu.with_memory_space_constraint(at, pltpu.VMEM)

    acc = None
    for place, s in enumerate(order):
        last = place == phases - 1
        acc = match(blocks, s, length, own_blocks, last, codes, counts, at, arrays[place], acc)
    matched, prob = acc
    return matched, prob.reshape(-1)


def solution(mesh):
    placed = (
        P(None, AXES),
        P(AXES),
        P(AXES, None),
        P(AXES, None),
        P(AXES, None),
        P(None, AXES),
        P(AXES),
        P(AXES),
        P(None, AXES),
    )
    return jax.shard_map(work, mesh=mesh, in_specs=placed, out_specs=(P(None, AXES), P(AXES)), check_vma=False)
```

time: 117 us -> 94.5 us (0.81)
  Pallas kernels: 67.2 us -> 47.5 us
  waiting for transfers between devices: 26.9 us -> 16.8 us
  starting transfers between devices: 17.4 us -> 21.5 us
  local copies, waits for them, and re-layouts: 3.18 us -> 5.5 us
    pallas_call x3 -> x6, Pallas kernels: 67.2 us -> 47.5 us  [the longest x4 34.2 us: match(): pl.pallas_call(functools.partial(match_kernel, blocks, place, length, spa...]
    ppermute x15, waiting for transfers between devices: 26.9 us -> 16.8 us  [send(): return lax.ppermute(array, AXES, pairs)]
    ppermute x15, starting transfers between devices: 17.4 us -> 21.5 us  [send(): return lax.ppermute(array, AXES, pairs)]
    unnamed x21 -> x22, local copies, waits for them, and re-layouts: 2.14 us -> 5.24 us
  transfers between devices with their start and end apart: 15 -> 15, of which waited for: 6 -> 4; matrix products, arithmetic and copies ran while one was open for 3% -> 1% of each run, Pallas kernels for 21% -> 39%
where the time goes in v2:
time: 94.5 us; the launch traced here: 94.1 us
  Pallas kernels  47.5 us (50%)
  starting transfers between devices  21.5 us (23%)
  waiting for transfers between devices  16.8 us (18%)
  local copies, waits for them, and re-layouts  5.5 us (6%)
  other arithmetic  1.94 us (2%)
    pallas_call x4, Pallas kernels, match(): pl.pallas_call(functools.partial(match_kernel, blocks, place, length, spa...  34.2 us
    ppermute x15, starting transfers between devices, send(): return lax.ppermute(array, AXES, pairs)  21.5 us
    ppermute x15, waiting for transfers between devices, send(): return lax.ppermute(array, AXES, pairs)  16.8 us
    pallas_call x1, Pallas kernels, work(): at = prep(a_coord, var_rows)  7.13 us
    pallas_call x1, Pallas kernels, work(): codes, counts = plan(entry.T.reshape(items // TB, TB))  6.17 us
    unnamed x22, local copies, waits for them, and re-layouts  5.24 us
  transfers between devices with their start and end apart: 15, of which 4 were waited for; matrix products, arithmetic and copies ran while one was open for 1% of the time, Pallas kernels for 39%

profile of v2, /device:TPU:1, one launch (start us, length us, event | category | flops | bytes accessed | tf_op | source)
XLA Modules:
  0.0 94.1 jit_solution(5140952209014813421)
XLA Ops:
  0.6 1.1 %pad_maximum_fusion.4 = f32[7,8192]{1,0:T(8,128)S(1)} fusion(f32[1,8192]{1,0:T(1,128)} %bitcast.12, f32[1,8192]{1,0:T(1,128)} %bitcast.13, f32[3,8192]{1,0:T(4,128)} %param.17, f32[2,8192]{1,0:T(2,128)} %param.14), kind=kLoop, calls=%fused_computation.4 | loop fusion | flops 172032 | bytes 458752 | tf_op jit(solution)/shard_map/concatenate | solution.py:266
  1.7 0.1 reshape.23
  1.8 2.1 %collective-permute-start.12 = (f32[448,128]{1,0:T(8,128)S(1)}, f32[448,128]{1,0:T(8,128)S(1)}, u32[]{:S(2)}, u32[]{:S(2)}) collective-permute-start(f32[448,128]{1,0:T(8,128)S(1)} %reshape.23), channel_id=1, source_target_pairs={{0,4},{1,3},{2,6},{3,1},{4,0},{5,7},{6,2},{7,5},{8,12},{9,11},{10,... | collective-permute-start | bytes 688136 | tf_op jit(solution)/shard_map/ppermute | solution.py:61
  4.0 1.3 %collective-permute-start = (f32[448,128]{1,0:T(8,128)S(1)}, f32[448,128]{1,0:T(8,128)S(1)}, u32[]{:S(2)}, u32[]{:S(2)}) collective-permute-start(f32[448,128]{1,0:T(8,128)S(1)} %reshape.23), channel_id=1, source_target_pairs={{0,8},{1,9},{2,10},{3,11},{4,12},{5,13},{6,14},{7,15},{8,16},{9,17... | collective-permute-start | bytes 688136 | tf_op jit(solution)/shard_map/ppermute | solution.py:61
  5.3 2.0 %collective-permute-start.5 = (f32[448,128]{1,0:T(8,128)S(1)}, f32[448,128]{1,0:T(8,128)S(1)}, u32[]{:S(2)}, u32[]{:S(2)}) collective-permute-start(f32[448,128]{1,0:T(8,128)S(1)} %reshape.23), channel_id=1, source_target_pairs={{0,24},{1,25},{2,26},{3,27},{4,28},{5,29},{6,30},{7,31},{8,0},{9,1... | collective-permute-start | bytes 688136 | tf_op jit(solution)/shard_map/ppermute | solution.py:61
  7.3 0.7 compare_reduce_fusion
  8.0 0.0 copy-start
  8.0 0.9 %copy-done = f32[2,32768]{1,0:T(2,128)S(1)} copy-done((f32[2,32768]{1,0:T(2,128)S(1)}, f32[2,32768]{1,0:T(2,128)}, u32[]{:S(2)}) %copy-start) | copy-done | bytes 262168
  8.9 0.9 copy-done.1
  9.9 7.1 %prep.1.at_ref = bf16[32768,48]{1,0:T(8,128)(2,1)S(1)} custom-call(f32[2,32768]{1,0:T(2,128)S(1)} %copy-done, f32[256,128]{1,0:T(8,128)S(1)} %bitcast.11), custom_call_target="tpu_custom_call" | custom-call | flops 4000000000 | bytes 10000000 | tf_op jit(solution)/shard_map/prep/pallas_call | solution.py:307
  17.0 3.2 %copy-done.2 = bf16[32768,48]{1,0:T(8,128)(2,1)} copy-done((bf16[32768,48]{1,0:T(8,128)(2,1)}, bf16[32768,48]{1,0:T(8,128)(2,1)S(1)}, u32[]{:S(2)}) %copy-start.2) | copy-done | bytes 3145752
  20.4 6.2 %plan.1 = (s32[5280]{0:T(1024)S(1)}, s32[8]{0:T(128)S(1)}) custom-call(s32[8,128]{1,0:T(8,128)S(1)} %reshape.21.entry_ref), custom_call_target="tpu_custom_call" | custom-call | flops 1000000000 | bytes 1000000 | tf_op jit(solution)/shard_map/plan/pallas_call | solution.py:295
  26.5 0.0 collective-permute-done.12
  26.6 1.3 %collective-permute-start.13 = (f32[896,128]{1,0:T(8,128)S(1)}, f32[896,128]{1,0:T(8,128)S(1)}, u32[]{:S(2)}, u32[]{:S(2)}) collective-permute-start(f32[896,128]{1,0:T(8,128)S(1)} %pad_maximum_fusion.3), channel_id=1, source_target_pairs={{0,2},{1,5},{2,0},{3,7},{4,6},{5,1},{6,4},{7,3},{8,10},{9,13},{10,... | collective-permute-start | bytes 1376264 | tf_op jit(solution)/shard_map/ppermute | solution.py:61
  27.9 0.0 collective-permute-done
  27.9 0.2 collective-permute-start.9
  28.1 1.3 %collective-permute-start.6 = (f32[448,128]{1,0:T(8,128)S(1)}, f32[448,128]{1,0:T(8,128)S(1)}, u32[]{:S(2)}, u32[]{:S(2)}) collective-permute-start(f32[448,128]{1,0:T(8,128)S(1)} %collective-permute-done.5), channel_id=1, source_target_pairs={{0,4},{1,3},{2,6},{3,1},{4,0},{5,7},{6,2},{7,5},{8,12},{9,11},{10,... | collective-permute-start | bytes 688136 | tf_op jit(solution)/shard_map/ppermute | solution.py:61
  29.5 5.3 %collective-permute-done.9 = f32[448,128]{1,0:T(8,128)S(1)} collective-permute-done((f32[448,128]{1,0:T(8,128)S(1)}, f32[448,128]{1,0:T(8,128)S(1)}, u32[]{:S(2)}, u32[]{:S(2)}) %collective-permute-start.9) | collective-permute-done | bytes 229408 | tf_op jit(solution)/shard_map/ppermute | solution.py:61
  34.8 0.5 collective-permute-start.10
  35.4 4.3 %collective-permute-done.6 = f32[448,128]{1,0:T(8,128)S(1)} collective-permute-done((f32[448,128]{1,0:T(8,128)S(1)}, f32[448,128]{1,0:T(8,128)S(1)}, u32[]{:S(2)}, u32[]{:S(2)}) %collective-permute-start.6) | collective-permute-done | bytes 229408 | tf_op jit(solution)/shard_map/ppermute | solution.py:61
  39.8 0.5 collective-permute-start.7
  40.4 3.7 %collective-permute-start.14 = (f32[1792,128]{1,0:T(8,128)S(1)}, f32[1792,128]{1,0:T(8,128)S(1)}, u32[]{:S(2)}, u32[]{:S(2)}) collective-permute-start(f32[1792,128]{1,0:T(8,128)S(1)} %constant_dynamic-update-slice_fusion.9.refs_0_), channel_id=1, source_target_pairs={{0,1},{1,0},{2,3},{3,2},{4,5},{5,4},{6,7},{7,6},{8,9},{9,8},{10,11... | collective-permute-start | bytes 2752520 | tf_op jit(solution)/shard_map/ppermute | solution.py:61
  44.0 3.9 %collective-permute-done.2 = f32[448,128]{1,0:T(8,128)S(1)} collective-permute-done((f32[448,128]{1,0:T(8,128)S(1)}, f32[448,128]{1,0:T(8,128)S(1)}, u32[]{:S(2)}, u32[]{:S(2)}) %collective-permute-start.2) | collective-permute-done | bytes 229408 | tf_op jit(solution)/shard_map/ppermute | solution.py:61
  48.0 1.1 %collective-permute-start.3 = (f32[896,128]{1,0:T(8,128)S(1)}, f32[896,128]{1,0:T(8,128)S(1)}, u32[]{:S(2)}, u32[]{:S(2)}) collective-permute-start(f32[896,128]{1,0:T(8,128)S(1)} %pad_maximum_fusion), channel_id=1, source_target_pairs={{0,2},{1,5},{2,0},{3,7},{4,6},{5,1},{6,4},{7,3},{8,10},{9,13},{10,... | collective-permute-start | bytes 1376264 | tf_op jit(solution)/shard_map/ppermute | solution.py:61
  49.1 3.1 %collective-permute-start.11 = (f32[1792,128]{1,0:T(8,128)S(1)}, f32[1792,128]{1,0:T(8,128)S(1)}, u32[]{:S(2)}, u32[]{:S(2)}) collective-permute-start(f32[1792,128]{1,0:T(8,128)S(1)} %constant_dynamic-update-slice_fusion.6.refs_0_), channel_id=1, source_target_pairs={{0,1},{1,0},{2,3},{3,2},{4,5},{5,4},{6,7},{7,6},{8,9},{9,8},{10,11... | collective-permute-start | bytes 2752520 | tf_op jit(solution)/shard_map/ppermute | solution.py:61
  52.3 0.9 collective-permute-start.8
  53.2 3.2 %collective-permute-done.3 = f32[896,128]{1,0:T(8,128)S(1)} collective-permute-done((f32[896,128]{1,0:T(8,128)S(1)}, f32[896,128]{1,0:T(8,128)S(1)}, u32[]{:S(2)}, u32[]{:S(2)}) %collective-permute-start.3) | collective-permute-done | bytes 458784 | tf_op jit(solution)/shard_map/ppermute | solution.py:61
  56.4 3.4 %collective-permute-start.4 = (f32[1792,128]{1,0:T(8,128)S(1)}, f32[1792,128]{1,0:T(8,128)S(1)}, u32[]{:S(2)}, u32[]{:S(2)}) collective-permute-start(f32[1792,128]{1,0:T(8,128)S(1)} %constant_dynamic-update-slice_fusion.refs_0_), channel_id=1, source_target_pairs={{0,1},{1,0},{2,3},{3,2},{4,5},{5,4},{6,7},{7,6},{8,9},{9,8},{10,11... | collective-permute-start | bytes 2752520 | tf_op jit(solution)/shard_map/ppermute | solution.py:61
  59.9 9.2 %shard_map.104.refs_2_ = f32[257,8,128]{2,1,0:T(8,128)S(1)} custom-call(s32[5280]{0:T(1024)S(1)} %get-tuple-element.6.codes_ref, s32[8]{0:T(128)S(1)} %get-tuple-element.7.count_ref, bf16[32768,48]{1,0:T(8,128)(2,1)S(1)} %copy-done.3, f32[1792,128]{1,0:T(8,128)S(1)} %constant_dynamic-update-slice_fusion.9.refs_0_, ...), custom_call_target="tpu_custom_call" | custom-call | flops 4000000000 | bytes 10000000 | tf_op jit(solution)/shard_map/pallas_call | solution.py:240
  69.1 6.4 %shard_map.105.refs_2_ = f32[257,8,128]{2,1,0:T(8,128)S(1)} custom-call(s32[5280]{0:T(1024)S(1)} %get-tuple-element.6.codes_ref, s32[8]{0:T(128)S(1)} %get-tuple-element.7.count_ref, bf16[32768,48]{1,0:T(8,128)(2,1)S(1)} %copy-done.3, f32[1792,128]{1,0:T(8,128)S(1)} %constant_dynamic-update-slice_fusion.6.refs_0_, ...), custom_call_target="tpu_custom_call", output_to_operand_aliasing={{}: (5, {})} | custom-call | flops 4000000000 | bytes 10000000 | tf_op jit(solution)/shard_map/pallas_call | solution.py:240
  75.5 7.8 %shard_map.106.refs_2_ = f32[257,8,128]{2,1,0:T(8,128)S(1)} custom-call(s32[5280]{0:T(1024)S(1)} %get-tuple-element.6.codes_ref, s32[8]{0:T(128)S(1)} %get-tuple-element.7.count_ref, bf16[32768,48]{1,0:T(8,128)(2,1)S(1)} %copy-done.3, f32[1792,128]{1,0:T(8,128)S(1)} %constant_dynamic-update-slice_fusion.3.refs_0_, ...), custom_call_target="tpu_custom_call", output_to_operand_aliasing={{}: (5, {})} | custom-call | flops 4000000000 | bytes 10000000 | tf_op jit(solution)/shard_map/pallas_call | solution.py:240
  83.3 10.8 %shard_map.107 = (f32[5,32768]{1,0:T(8,128)}, f32[256,128]{1,0:T(8,128)}) custom-call(s32[5280]{0:T(1024)S(1)} %get-tuple-element.6.codes_ref, s32[8]{0:T(128)S(1)} %get-tuple-element.7.count_ref, bf16[32768,48]{1,0:T(8,128)(2,1)S(1)} %copy-done.3, f32[1792,128]{1,0:T(8,128)S(1)} %constant_dynamic-update-slice_fusion.refs_0_, ...), custom_call_target="tpu_custom_call" | custom-call | flops 4000000000 | bytes 10000000 | tf_op jit(solution)/shard_map/pallas_call | solution.py:240
  (41 shorter events, 0.5 us)
Async XLA Ops:
  1.8 24.7 %collective-permute-start.12 = (f32[448,128]{1,0:T(8,128)S(1)}, f32[448,128]{1,0:T(8,128)S(1)}, u32[]{:S(2)}, u32[]{:S(2)}) collective-permute-start(f32[448,128]{1,0:T(8,128)S(1)} %reshape.23), channel_id=1, source_target_pairs={{0,4},{1,3},{2,6},{3,1},{4,0},{5,7},{6,2},{7,5},{8,12},{9,11},{10,... | collective-permute-start | bytes 688136 | tf_op jit(solution)/shard_map/ppermute | solution.py:61
  4.0 23.9 %collective-permute-start = (f32[448,128]{1,0:T(8,128)S(1)}, f32[448,128]{1,0:T(8,128)S(1)}, u32[]{:S(2)}, u32[]{:S(2)}) collective-permute-start(f32[448,128]{1,0:T(8,128)S(1)} %reshape.23), channel_id=1, source_target_pairs={{0,8},{1,9},{2,10},{3,11},{4,12},{5,13},{6,14},{7,15},{8,16},{9,17... | collective-permute-start | bytes 688136 | tf_op jit(solution)/shard_map/ppermute | solution.py:61
  5.3 22.9 %collective-permute-start.5 = (f32[448,128]{1,0:T(8,128)S(1)}, f32[448,128]{1,0:T(8,128)S(1)}, u32[]{:S(2)}, u32[]{:S(2)}) collective-permute-start(f32[448,128]{1,0:T(8,128)S(1)} %reshape.23), channel_id=1, source_target_pairs={{0,24},{1,25},{2,26},{3,27},{4,28},{5,29},{6,30},{7,31},{8,0},{9,1... | collective-permute-start | bytes 688136 | tf_op jit(solution)/shard_map/ppermute | solution.py:61
  8.0 1.0 %copy-start = (f32[2,32768]{1,0:T(2,128)S(1)}, f32[2,32768]{1,0:T(2,128)}, u32[]{:S(2)}) copy-start(f32[2,32768]{1,0:T(2,128)} %coord_ref.1) | copy-start | bytes 786436
  8.9 0.9 copy-start.1
  9.8 10.4 %copy-start.5 = (s32[256,1]{0,1:T(1,128)S(1)}, s32[256,1]{0,1:T(1,128)}, u32[]{:S(2)}) copy-start(s32[256,1]{0,1:T(1,128)} %param.11) | copy-start | bytes 3076
  9.9 10.4 %copy-start.4 = (s32[256,4]{0,1:T(4,128)S(1)}, s32[256,4]{0,1:T(4,128)}, u32[]{:S(2)}) copy-start(s32[256,4]{0,1:T(4,128)} %param.12) | copy-start | bytes 12292
  9.9 10.4 %copy-start.6 = (s32[256,1]{0,1:T(1,128)S(1)}, s32[256,1]{0,1:T(1,128)}, u32[]{:S(2)}) copy-start(s32[256,1]{0,1:T(1,128)} %param.13) | copy-start | bytes 3076
  17.0 3.3 %copy-start.2 = (bf16[32768,48]{1,0:T(8,128)(2,1)}, bf16[32768,48]{1,0:T(8,128)(2,1)S(1)}, u32[]{:S(2)}) copy-start(bf16[32768,48]{1,0:T(8,128)(2,1)S(1)} %prep.1.at_ref) | copy-start | bytes 9437188
  26.6 13.7 %collective-permute-start.13 = (f32[896,128]{1,0:T(8,128)S(1)}, f32[896,128]{1,0:T(8,128)S(1)}, u32[]{:S(2)}, u32[]{:S(2)}) collective-permute-start(f32[896,128]{1,0:T(8,128)S(1)} %pad_maximum_fusion.3), channel_id=1, source_target_pairs={{0,2},{1,5},{2,0},{3,7},{4,6},{5,1},{6,4},{7,3},{8,10},{9,13},{10,... | collective-permute-start | bytes 1376264 | tf_op jit(solution)/shard_map/ppermute | solution.py:61
  27.9 7.0 %collective-permute-start.9 = (f32[448,128]{1,0:T(8,128)S(1)}, f32[448,128]{1,0:T(8,128)S(1)}, u32[]{:S(2)}, u32[]{:S(2)}) collective-permute-start(f32[448,128]{1,0:T(8,128)S(1)} %collective-permute-done), channel_id=1, source_target_pairs={{0,4},{1,3},{2,6},{3,1},{4,0},{5,7},{6,2},{7,5},{8,12},{9,11},{10,... | collective-permute-start | bytes 688136 | tf_op jit(solution)/shard_map/ppermute | solution.py:61
  28.1 12.2 %collective-permute-start.1 = (f32[448,128]{1,0:T(8,128)S(1)}, f32[448,128]{1,0:T(8,128)S(1)}, u32[]{:S(2)}, u32[]{:S(2)}) collective-permute-start(f32[448,128]{1,0:T(8,128)S(1)} %collective-permute-done), channel_id=1, source_target_pairs={{0,8},{1,9},{2,10},{3,11},{4,12},{5,13},{6,14},{7,15},{8,16},{9,17... | collective-permute-start | bytes 688136 | tf_op jit(solution)/shard_map/ppermute | solution.py:61
  28.1 11.6 %collective-permute-start.6 = (f32[448,128]{1,0:T(8,128)S(1)}, f32[448,128]{1,0:T(8,128)S(1)}, u32[]{:S(2)}, u32[]{:S(2)}) collective-permute-start(f32[448,128]{1,0:T(8,128)S(1)} %collective-permute-done.5), channel_id=1, source_target_pairs={{0,4},{1,3},{2,6},{3,1},{4,0},{5,7},{6,2},{7,5},{8,12},{9,11},{10,... | collective-permute-start | bytes 688136 | tf_op jit(solution)/shard_map/ppermute | solution.py:61
  29.4 30.4 %copy-start.3 = (bf16[32768,48]{1,0:T(8,128)(2,1)S(1)}, bf16[32768,48]{1,0:T(8,128)(2,1)}, u32[]{:S(2)}) copy-start(bf16[32768,48]{1,0:T(8,128)(2,1)} %copy-done.2) | copy-start | bytes 9437188
  34.8 14.2 %collective-permute-start.10 = (f32[896,128]{1,0:T(8,128)S(1)}, f32[896,128]{1,0:T(8,128)S(1)}, u32[]{:S(2)}, u32[]{:S(2)}) collective-permute-start(f32[896,128]{1,0:T(8,128)S(1)} %pad_maximum_fusion.2), channel_id=1, source_target_pairs={{0,2},{1,5},{2,0},{3,7},{4,6},{5,1},{6,4},{7,3},{8,10},{9,13},{10,... | collective-permute-start | bytes 1376264 | tf_op jit(solution)/shard_map/ppermute | solution.py:61
  39.8 12.4 %collective-permute-start.7 = (f32[896,128]{1,0:T(8,128)S(1)}, f32[896,128]{1,0:T(8,128)S(1)}, u32[]{:S(2)}, u32[]{:S(2)}) collective-permute-start(f32[896,128]{1,0:T(8,128)S(1)} %pad_maximum_fusion.1), channel_id=1, source_target_pairs={{0,2},{1,5},{2,0},{3,7},{4,6},{5,1},{6,4},{7,3},{8,10},{9,13},{10,... | collective-permute-start | bytes 1376264 | tf_op jit(solution)/shard_map/ppermute | solution.py:61
  40.3 7.6 %collective-permute-start.2 = (f32[448,128]{1,0:T(8,128)S(1)}, f32[448,128]{1,0:T(8,128)S(1)}, u32[]{:S(2)}, u32[]{:S(2)}) collective-permute-start(f32[448,128]{1,0:T(8,128)S(1)} %collective-permute-done.1), channel_id=1, source_target_pairs={{0,4},{1,3},{2,6},{3,1},{4,0},{5,7},{6,2},{7,5},{8,12},{9,11},{10,... | collective-permute-start | bytes 688136 | tf_op jit(solution)/shard_map/ppermute | solution.py:61
  40.4 19.5 %collective-permute-start.14 = (f32[1792,128]{1,0:T(8,128)S(1)}, f32[1792,128]{1,0:T(8,128)S(1)}, u32[]{:S(2)}, u32[]{:S(2)}) collective-permute-start(f32[1792,128]{1,0:T(8,128)S(1)} %constant_dynamic-update-slice_fusion.9.refs_0_), channel_id=1, source_target_pairs={{0,1},{1,0},{2,3},{3,2},{4,5},{5,4},{6,7},{7,6},{8,9},{9,8},{10,11... | collective-permute-start | bytes 2752520 | tf_op jit(solution)/shard_map/ppermute | solution.py:61
  48.0 8.4 %collective-permute-start.3 = (f32[896,128]{1,0:T(8,128)S(1)}, f32[896,128]{1,0:T(8,128)S(1)}, u32[]{:S(2)}, u32[]{:S(2)}) collective-permute-start(f32[896,128]{1,0:T(8,128)S(1)} %pad_maximum_fusion), channel_id=1, source_target_pairs={{0,2},{1,5},{2,0},{3,7},{4,6},{5,1},{6,4},{7,3},{8,10},{9,13},{10,... | collective-permute-start | bytes 1376264 | tf_op jit(solution)/shard_map/ppermute | solution.py:61
  49.1 20.0 %collective-permute-start.11 = (f32[1792,128]{1,0:T(8,128)S(1)}, f32[1792,128]{1,0:T(8,128)S(1)}, u32[]{:S(2)}, u32[]{:S(2)}) collective-permute-start(f32[1792,128]{1,0:T(8,128)S(1)} %constant_dynamic-update-slice_fusion.6.refs_0_), channel_id=1, source_target_pairs={{0,1},{1,0},{2,3},{3,2},{4,5},{5,4},{6,7},{7,6},{8,9},{9,8},{10,11... | collective-permute-start | bytes 2752520 | tf_op jit(solution)/shard_map/ppermute | solution.py:61
  52.3 23.2 %collective-permute-start.8 = (f32[1792,128]{1,0:T(8,128)S(1)}, f32[1792,128]{1,0:T(8,128)S(1)}, u32[]{:S(2)}, u32[]{:S(2)}) collective-permute-start(f32[1792,128]{1,0:T(8,128)S(1)} %constant_dynamic-update-slice_fusion.3.refs_0_), channel_id=1, source_target_pairs={{0,1},{1,0},{2,3},{3,2},{4,5},{5,4},{6,7},{7,6},{8,9},{9,8},{10,11... | collective-permute-start | bytes 2752520 | tf_op jit(solution)/shard_map/ppermute | solution.py:61
  56.4 26.8 %collective-permute-start.4 = (f32[1792,128]{1,0:T(8,128)S(1)}, f32[1792,128]{1,0:T(8,128)S(1)}, u32[]{:S(2)}, u32[]{:S(2)}) collective-permute-start(f32[1792,128]{1,0:T(8,128)S(1)} %constant_dynamic-update-slice_fusion.refs_0_), channel_id=1, source_target_pairs={{0,1},{1,0},{2,3},{3,2},{4,5},{5,4},{6,7},{7,6},{8,9},{9,8},{10,11... | collective-permute-start | bytes 2752520 | tf_op jit(solution)/shard_map/ppermute | solution.py:61

commit v3 on v2

--- a/solution.py
+++ b/solution.py
@@ -18,6 +18,7 @@
 HALF_LOG2E = 0.5 * math.log2(math.e)
 AXES = ("zone", "tile")
 VMEM = pl.BlockSpec(memory_space=pltpu.VMEM)
+HBM = pl.BlockSpec(memory_space=pltpu.HBM)
 SMEM = pl.BlockSpec(memory_space=pltpu.SMEM)
 
 
@@ -63,36 +64,72 @@
 
 def gather_phases(own, grid):
     n = grid.high
-    held = {0: own}
-    order = [0]
-    for step in range(1, n // 2 + 1):
-        for s, back in ((step, 1), (n - step, -1)):
-            if s not in held:
-                held[s] = send(held[(s - back) % n], grid.shift(back))
-                order.append(s)
+    join = lambda parts: jnp.concatenate(parts, axis=0) if len(parts) > 1 else parts[0]
+    up = down = join([own, send(own, grid.side(True))])
     phases = []
-    for s in order:
-        z = held[s]
-        pair = jnp.concatenate([z, send(z, grid.side(True))], axis=0)
-        four = jnp.concatenate([pair, send(pair, grid.side(False))], axis=0)
-        phases.append((four, send(four, grid.core())))
-    return phases, order
+    for g in range(n // 2 + 1):
+        pairs = [up]
+        if g == 1:
+            z = send(own, grid.shift(1))
+            pairs = [join([z, send(z, grid.side(True))])]
+        elif g > 1:
+            pairs = [send(up, grid.shift(1))]
+        if g > 0 and 2 * g != n:
+            pairs.append(send(down, grid.shift(-1)))
+        up, down = pairs[0], pairs[-1]
+        near = join(pairs)
+        across = send(near, grid.side(False))
+        phases.append((near, across, send(near, grid.core()), send(across, grid.core())))
+    return phases
 
 
 def locate(zone, tile, block, grid, rows):
     my_zone, my_tile = lax.axis_index("zone"), lax.axis_index("tile")
-    distance = lax.rem((my_zone >> 1) - (zone >> 1) + grid.high, grid.high)
+    n = grid.high
+    distance = (my_zone >> 1) - (zone >> 1)
+    distance = jnp.where(distance < 0, distance + n, distance)
+    phase = jnp.minimum(distance, n - distance)
+    back = jnp.where(distance == phase, 0, 1)
     dx = (zone & 1) ^ (my_zone & 1)
     dy = ((tile >> 1) ^ (my_tile >> 1)) & 1
     dc = (tile ^ my_tile) & 1
-    place = jnp.where((tile & 1) == 0, dx + 2 * dy, dy + 2 * dx)
-    return distance, (dc << 16) | (place * rows + block)
-
-
-def plan_kernel(phases, length, dummy, entry_ref, codes_ref, count_ref, place_ref, work_ref, sem):
-    entry = entry_ref[...]
+    first = jnp.where((tile & 1) == 0, dx, dy)
+    return phase, ((2 * dc + (dx + dy - first)) << 16) | ((2 * back + first) * rows + block)
+
+
+def plan_kernel(grid, own_blocks, phases, length, *refs):
+    *inputs, codes_ref, count_ref, dest_ref, cand_ref, live_ref, place_ref, work_ref, sems = refs
+    copies = [
+        pltpu.make_async_copy(a, b, sems.at[i]) for i, (a, b) in enumerate(zip(inputs, (dest_ref, cand_ref, live_ref)))
+    ]
+    for copy in copies:
+        copy.start()
+    for copy in copies:
+        copy.wait()
+    cand = cand_ref[...]
+    _, blocks = cand.shape
+    zones, tiles = grid.zones, grid.tiles
+    rows = NQ * own_blocks
+    dest = jnp.broadcast_to(dest_ref[...], cand.shape)
+    home = jnp.zeros_like(cand)
+    for z in range(1, zones):
+        home = home + jnp.where(dest >= z * tiles, 1, 0)
+    tile = dest - home * tiles
+    shift = jnp.where(cand >= MB, 1, 0) + jnp.where(cand >= MB + own_blocks, 1, 0) - 1
+    zone = home + shift
+    block = cand - MB - shift * own_blocks
+    slot = lax.broadcasted_iota(jnp.int32, cand.shape, 0)
+    here = lax.broadcasted_iota(jnp.int32, cand.shape, 1)
+    live = (slot < live_ref[...]) & (zone >= 0) & (zone < zones)
+    if phases > 1:
+        phase, code = locate(zone, tile, block, grid, rows)
+    else:
+        phase, code = jnp.zeros_like(zone), (zone * tiles + tile) * rows + block
+    entry = jnp.where(live, (phase << 28) | (here << 18) | code, phases << 28)
+    entry = jnp.concatenate([entry[:, g * TB : (g + 1) * TB] for g in range(blocks // TB)], axis=0)
+
     high = entry.shape[0]
-    phase = entry >> 27
+    phase = entry >> 28
     lanes = (TB, TB)
     earlier = lax.broadcasted_iota(jnp.int32, lanes, 0) < lax.broadcasted_iota(jnp.int32, lanes, 1)
     sums = jnp.concatenate([jnp.where(earlier, 1.0, 0.0), jnp.ones(lanes, F32)], axis=1).astype(BF)
@@ -104,32 +141,30 @@
         member = jnp.where(phase == p, 1.0, 0.0)
         both = jnp.dot(member.astype(BF), sums, preferred_element_type=F32)
         before, total = both[:, :TB], both[:, TB:]
-        rows = jnp.dot(above, total.astype(BF), preferred_element_type=F32)
-        place = place + jnp.where(phase == p, (before + rows).astype(jnp.int32), 0)
+        ahead = jnp.dot(above, total.astype(BF), preferred_element_type=F32)
+        place = place + jnp.where(phase == p, (before + ahead).astype(jnp.int32), 0)
         totals.append(jnp.sum(total, axis=0, keepdims=True).astype(jnp.int32))
     place_ref[pl.ds(0, high), :] = place
-    place_ref[pl.ds(high, high), :] = entry & ((1 << 27) - 1)
+    place_ref[pl.ds(high, high), :] = entry & ((1 << 28) - 1)
     place_ref[pl.ds(2 * high, 8), :] = jnp.concatenate(
         totals + [jnp.zeros((1, TB), jnp.int32)] * (7 - phases), axis=0
     )
-    copy = pltpu.make_async_copy(place_ref, work_ref, sem)
+    copy = pltpu.make_async_copy(place_ref, work_ref, sems.at[3])
     copy.start()
     copy.wait()
 
     def row(r, _):
-        def step(i, _):
-            for t in range(16):
-                codes_ref[work_ref[r, i * 16 + t]] = work_ref[high + r, i * 16 + t]
-            return 0
-
-        return lax.fori_loop(0, TB // 16, step, 0)
+        for first in range(0, TB, 8):
+            lanes = range(first, first + 8)
+            places = [work_ref[r, t] for t in lanes]
+            values = [work_ref[high + r, t] for t in lanes]
+            for p, v in zip(places, values):
+                codes_ref[p] = v
+        return 0
 
     lax.fori_loop(0, high, row, 0)
     for p in range(phases):
-        count = work_ref[2 * high + p, 0]
-        for t in range(UNROLL):
-            codes_ref[p * length + count + t] = jnp.int32(dummy)
-        count_ref[p] = count
+        count_ref[p] = work_ref[2 * high + p, 0]
 
 
 def prep_kernel(blocks, coord_ref, var_ref, at_ref):
@@ -138,36 +173,40 @@
     ).astype(BF)
     row = lax.broadcasted_iota(jnp.int32, (8, TB), 0)
 
+    def stack(block):
+        lanes = pl.ds(pl.multiple_of(block * TB, TB), TB)
+        u, v = coord_ref[0:1, lanes], coord_ref[1:2, lanes]
+        s = var_ref[pl.ds(block, 1), :]
+        q = -HALF_LOG2E * (u * u + v * v)
+        tile = jnp.where(row == 3, q, jnp.where(row == 4, s, jnp.where(row == 2, 1.0, 0.0)))
+        tile = jnp.where(row == 0, u, jnp.where(row == 1, v, tile))
+        h, m, l = split3(tile)
+        return [h, h, m, m, h, l]
+
     def step(i, _):
         for t in range(8):
-            block = i * 8 + t
-            lanes = pl.ds(pl.multiple_of(block * TB, TB), TB)
-            u, v = coord_ref[0:1, lanes], coord_ref[1:2, lanes]
-            s = var_ref[pl.ds(block, 1), :]
-            q = -HALF_LOG2E * (u * u + v * v)
-            tile = jnp.where(row == 3, q, jnp.where(row == 4, s, jnp.where(row == 2, 1.0, 0.0)))
-            tile = jnp.where(row == 0, u, jnp.where(row == 1, v, tile))
-            h, m, l = split3(tile)
-            stack = jnp.concatenate([h, h, m, m, h, l], axis=0).astype(BF)
-            turned = lax.dot_general(eye, stack, (((1,), (1,)), ((), ())), preferred_element_type=F32)
-            at_ref[lanes, :] = turned.astype(BF)
+            pair = i * 8 + t
+            both = jnp.concatenate(stack(2 * pair) + stack(2 * pair + 1), axis=0).astype(BF)
+            turned = lax.dot_general(eye, both, (((1,), (1,)), ((), ())), preferred_element_type=F32)
+            at_ref[pl.ds(pl.multiple_of(pair * TB, TB), TB), :] = turned.astype(BF)
         return 0
 
-    lax.fori_loop(0, blocks // 8, step, 0)
-
-
-def match_items(codes_ref, first, count, spacing, at_ref, b_refs, acc_ref):
+    lax.fori_loop(0, blocks // 16, step, 0)
+
+
+def match_items(codes_ref, first, count, dummy, spacing, at_ref, b_refs, acc_ref):
     row = lax.broadcasted_iota(jnp.int32, (8, TB), 0)
     gap = jnp.zeros((8 - NQ, TB), F32)
 
     def step(i, _):
         sums = []
         for t in range(UNROLL):
-            code = codes_ref[first + i * UNROLL + t]
-            block, half, start = code >> 17, (code >> 16) & 1, code & 0xFFFF
+            item = i * UNROLL + t
+            code = jnp.where(item < count, codes_ref[first + item], dummy)
+            block, which, start = code >> 18, (code >> 16) & 3, code & 0xFFFF
             x = b_refs[0][pl.ds(start, NQ, stride=spacing), :]
-            if len(b_refs) > 1:
-                x = jnp.where(half == 1, b_refs[1][pl.ds(start, NQ, stride=spacing), :], x)
+            for k in range(1, len(b_refs)):
+                x = jnp.where(which == k, b_refs[k][pl.ds(start, NQ, stride=spacing), :], x)
             x = jnp.concatenate([x, gap], axis=0)
             u, v, s, p = x[0:1], x[1:2], x[VAR : VAR + 1], x[PRIOR : PRIOR + 1]
             q = -HALF_LOG2E * (u * u + v * v)
@@ -175,8 +214,10 @@
             near = jnp.where(row < 2, x * (2 * HALF_LOG2E), near)
             spread = jnp.where(row == 2, s, jnp.where(row == 4, 1.0, 0.0))
             h, m, l = split3(jnp.concatenate([near, spread], axis=1))
-            stack = jnp.concatenate([h, m, h, m, l, h], axis=0).astype(BF)
-            held = jnp.minimum(block, at_ref.shape[0] // TB - 1)
+            even = [jnp.where((block & 1) == 0, part, 0.0) for part in (h, m, l)]
+            odd = [jnp.where((block & 1) == 0, 0.0, part) for part in (h, m, l)]
+            stack = jnp.concatenate([a[k] for a in (even, odd) for k in (0, 1, 0, 1, 2, 0)], axis=0).astype(BF)
+            held = jnp.minimum(block >> 1, at_ref.shape[0] // TB - 1)
             a = at_ref[pl.ds(pl.multiple_of(held * TB, TB), TB), :]
             both = jnp.dot(a, stack, preferred_element_type=F32)
             r = 1.0 / both[:, TB:]
@@ -216,7 +257,7 @@
         acc_ref[...] = refs.pop()[...]
     else:
         refs.pop()
-    match_items(codes_ref, place * length, count_ref[place], spacing, at_ref, refs, acc_ref)
+    match_items(codes_ref, place * length, count_ref[place], blocks << 18, spacing, at_ref, refs, acc_ref)
     if not last:
         return
 
@@ -258,46 +299,40 @@
     fast = is_grid({"zone": zones, "tile": tiles})
     grid = Grid(zones, tiles)
 
-    shift = (cand >= MB).astype(jnp.int32) + (cand >= MB + own_blocks).astype(jnp.int32) - 1
-    zone = dest // tiles + shift
-    tile = dest % tiles
-    block = cand - MB - shift * own_blocks
-    live = (jnp.arange(slots, dtype=jnp.int32)[None, :] < cand_count) & (zone >= 0) & (zone < zones)
     own = jnp.concatenate([b_coord, b_flux, b_var[None, :], b_prior[None, :]], axis=0).reshape(rows, TB)
     if fast:
-        arrays, order = gather_phases(own, grid)
-        phase, code = locate(zone, tile, block, grid, rows)
+        arrays = gather_phases(own, grid)
     else:
-        arrays, order = [(lax.all_gather(own, AXES, axis=0, tiled=True),)], [0]
-        phase, code = jnp.zeros_like(zone), (zone * tiles + tile) * rows + block
-    phases = len(order)
-    here = jnp.arange(blocks, dtype=jnp.int32)[:, None]
-    entry = jnp.where(live, (phase << 27) | (here << 17) | code, phases << 27)
+        arrays = [(lax.all_gather(own, AXES, axis=0, tiled=True),)]
+    phases = len(arrays)
     items = blocks * slots
     length = items + UNROLL
     plan = pl.pallas_call(
-        functools.partial(plan_kernel, phases, length, blocks << 17),
+        functools.partial(plan_kernel, grid, own_blocks, phases, length),
         out_shape=(
             jax.ShapeDtypeStruct(((phases + 1) * length,), jnp.int32),
             jax.ShapeDtypeStruct((8,), jnp.int32),
         ),
-        in_specs=[VMEM],
+        in_specs=[HBM, HBM, HBM],
         out_specs=(SMEM, SMEM),
         scratch_shapes=[
+            pltpu.VMEM((1, blocks), jnp.int32),
+            pltpu.VMEM((slots, blocks), jnp.int32),
+            pltpu.VMEM((1, blocks), jnp.int32),
             pltpu.VMEM((2 * items // TB + 8, TB), jnp.int32),
             pltpu.SMEM((2 * items // TB + 8, TB), jnp.int32),
-            pltpu.SemaphoreType.DMA(()),
+            pltpu.SemaphoreType.DMA((4,)),
         ],
         compiler_params=params(4),
         cost_estimate=pl.CostEstimate(flops=10**9, transcendentals=0, bytes_accessed=10**6),
         name="plan",
     )
-    codes, counts = plan(entry.T.reshape(items // TB, TB))
+    codes, counts = plan(*(pltpu.with_memory_space_constraint(x.T, pltpu.HBM) for x in (dest, cand, cand_count)))
 
     var_rows = a_var.reshape(blocks, TB)
     prep = pl.pallas_call(
         functools.partial(prep_kernel, blocks),
-        out_shape=jax.ShapeDtypeStruct((blocks * TB, 48), BF),
+        out_shape=jax.ShapeDtypeStruct((blocks // 2 * TB, 96), BF),
         in_specs=[VMEM, VMEM],
         out_specs=VMEM,
         compiler_params=params(4),
@@ -308,9 +343,9 @@
     at = pltpu.with_memory_space_constraint(at, pltpu.VMEM)
 
     acc = None
-    for place, s in enumerate(order):
+    for place in range(phases):
         last = place == phases - 1
-        acc = match(blocks, s, length, own_blocks, last, codes, counts, at, arrays[place], acc)
+        acc = match(blocks, place, length, own_blocks, last, codes, counts, at, arrays[place], acc)
     matched, prob = acc
     return matched, prob.reshape(-1)
 

time: 94.5 us -> 86.5 us (0.915)
  waiting for transfers between devices: 16.8 us -> 26.8 us
  starting transfers between devices: 21.5 us -> 15.1 us
  local copies, waits for them, and re-layouts: 5.5 us -> 0.22 us
  Pallas kernels: 47.5 us -> 42.3 us
    ppermute x15 -> x14, waiting for transfers between devices: 16.8 us -> 26.8 us  [send(): return lax.ppermute(array, AXES, pairs)]
    ppermute x15 -> x14, starting transfers between devices: 21.5 us -> 15.1 us  [send(): return lax.ppermute(array, AXES, pairs)]
    unnamed x22 -> x7, local copies, waits for them, and re-layouts: 5.24 us -> 0.06 us
    pallas_call x1, Pallas kernels: 7.13 us -> 4.38 us  [work(): at = prep(a_coord, var_rows)]
    pallas_call x1, Pallas kernels: 6.17 us -> 4.61 us  [work(): plan(*(pltpu.with_memory_space_constraint(x.T, pltpu.HBM) for x in (dest,...]
    pallas_call x4 -> x3, Pallas kernels: 34.2 us -> 33.3 us  [match(): pl.pallas_call(functools.partial(match_kernel, blocks, place, length, spa...]
  transfers between devices with their start and end apart: 15 -> 14, of which waited for: 4 -> 6; matrix products, arithmetic and copies ran while one was open for 1% -> 0% of each run, Pallas kernels for 39% -> 37%
where the time goes in v3:
time: 86.5 us; the launch traced here: 86.3 us
  Pallas kernels  42.3 us (49%)
  waiting for transfers between devices  26.8 us (31%)
  starting transfers between devices  15.1 us (17%)
  other arithmetic  1.1 us (1%)
    pallas_call x3, Pallas kernels, match(): pl.pallas_call(functools.partial(match_kernel, blocks, place, length, spa...  33.3 us
    ppermute x14, waiting for transfers between devices, send(): return lax.ppermute(array, AXES, pairs)  26.8 us
    ppermute x14, starting transfers between devices, send(): return lax.ppermute(array, AXES, pairs)  15.1 us
    pallas_call x1, Pallas kernels, work(): plan(*(pltpu.with_memory_space_constraint(x.T, pltpu.HBM) for x in (dest,...  4.61 us
    pallas_call x1, Pallas kernels, work(): at = prep(a_coord, var_rows)  4.38 us
  transfers between devices with their start and end apart: 14, of which 6 were waited for; matrix products, arithmetic and copies ran while one was open for 0% of the time, Pallas kernels for 37%

profile of v3, /device:TPU:1, one launch (start us, length us, event | category | flops | bytes accessed | tf_op | source)
XLA Modules:
  0.0 86.3 jit_solution(11163883446739587676)
XLA Ops:
  0.6 1.1 %pad_maximum_fusion.1 = f32[7,8192]{1,0:T(8,128)S(1)} fusion(f32[1,8192]{1,0:T(1,128)} %bitcast.8, f32[1,8192]{1,0:T(1,128)} %bitcast.9, f32[3,8192]{1,0:T(4,128)} %param.17, f32[2,8192]{1,0:T(2,128)} %param.14), kind=kLoop, calls=%fused_computation.1 | loop fusion | flops 172032 | bytes 458752 | tf_op jit(solution)/shard_map/concatenate | solution.py:302
  1.7 0.1 reshape.14
  1.8 2.1 %collective-permute-start.6 = (f32[448,128]{1,0:T(8,128)S(1)}, f32[448,128]{1,0:T(8,128)S(1)}, u32[]{:S(2)}, u32[]{:S(2)}) collective-permute-start(f32[448,128]{1,0:T(8,128)S(1)} %reshape.14), channel_id=1, source_target_pairs={{0,4},{1,3},{2,6},{3,1},{4,0},{5,7},{6,2},{7,5},{8,12},{9,11},{10,... | collective-permute-start | bytes 688136 | tf_op jit(solution)/shard_map/ppermute | solution.py:62
  4.0 1.3 %collective-permute-start = (f32[448,128]{1,0:T(8,128)S(1)}, f32[448,128]{1,0:T(8,128)S(1)}, u32[]{:S(2)}, u32[]{:S(2)}) collective-permute-start(f32[448,128]{1,0:T(8,128)S(1)} %reshape.14), channel_id=1, source_target_pairs={{0,8},{1,9},{2,10},{3,11},{4,12},{5,13},{6,14},{7,15},{8,16},{9,17... | collective-permute-start | bytes 688136 | tf_op jit(solution)/shard_map/ppermute | solution.py:62
  5.3 2.4 %collective-permute-done.6 = f32[448,128]{1,0:T(8,128)S(1)} collective-permute-done((f32[448,128]{1,0:T(8,128)S(1)}, f32[448,128]{1,0:T(8,128)S(1)}, u32[]{:S(2)}, u32[]{:S(2)}) %collective-permute-start.6) | collective-permute-done | bytes 229408 | tf_op jit(solution)/shard_map/ppermute | solution.py:62
  7.7 3.6 %collective-permute-start.7 = (f32[896,128]{1,0:T(8,128)S(1)}, f32[896,128]{1,0:T(8,128)S(1)}, u32[]{:S(2)}, u32[]{:S(2)}) collective-permute-start(f32[896,128]{1,0:T(8,128)S(1)} %constant_dynamic-update-slice_fusion.refs_0_), channel_id=1, source_target_pairs={{0,24},{1,25},{2,26},{3,27},{4,28},{5,29},{6,30},{7,31},{8,0},{9,1... | collective-permute-start | bytes 1376264 | tf_op jit(solution)/shard_map/ppermute | solution.py:62
  11.3 0.8 collective-permute-done
  12.1 0.4 collective-permute-start.1
  12.5 4.7 %collective-permute-done.1 = f32[448,128]{1,0:T(8,128)S(1)} collective-permute-done((f32[448,128]{1,0:T(8,128)S(1)}, f32[448,128]{1,0:T(8,128)S(1)}, u32[]{:S(2)}, u32[]{:S(2)}) %collective-permute-start.1) | collective-permute-done | bytes 229408 | tf_op jit(solution)/shard_map/ppermute | solution.py:62
  17.3 5.9 %collective-permute-done.7 = f32[896,128]{1,0:T(8,128)S(1)} collective-permute-done((f32[896,128]{1,0:T(8,128)S(1)}, f32[896,128]{1,0:T(8,128)S(1)}, u32[]{:S(2)}, u32[]{:S(2)}) %collective-permute-start.7) | collective-permute-done | bytes 458784 | tf_op jit(solution)/shard_map/ppermute | solution.py:62
  23.2 1.3 %collective-permute-start.8 = (f32[1792,128]{1,0:T(8,128)S(1)}, f32[1792,128]{1,0:T(8,128)S(1)}, u32[]{:S(2)}, u32[]{:S(2)}) collective-permute-start(f32[1792,128]{1,0:T(8,128)S(1)} %constant_dynamic-update-slice_fusion.2.refs_0_), channel_id=1, source_target_pairs={{0,2},{1,5},{2,0},{3,7},{4,6},{5,1},{6,4},{7,3},{8,10},{9,13},{10,... | collective-permute-start | bytes 2752520 | tf_op jit(solution)/shard_map/ppermute | solution.py:62
  24.5 0.3 collective-permute-start.11
  24.8 0.1 collective-permute-start.2
  24.8 1.6 %collective-permute-start.9 = (f32[1792,128]{1,0:T(8,128)S(1)}, f32[1792,128]{1,0:T(8,128)S(1)}, u32[]{:S(2)}, u32[]{:S(2)}) collective-permute-start(f32[1792,128]{1,0:T(8,128)S(1)} %constant_dynamic-update-slice_fusion.2.refs_0_), channel_id=1, source_target_pairs={{0,1},{1,0},{2,3},{3,2},{4,5},{5,4},{6,7},{7,6},{8,9},{9,8},{10,11... | collective-permute-start | bytes 2752520 | tf_op jit(solution)/shard_map/ppermute | solution.py:62
  26.4 9.4 %collective-permute-done.8.refs_1_ = f32[1792,128]{1,0:T(8,128)S(1)} collective-permute-done((f32[1792,128]{1,0:T(8,128)S(1)}, f32[1792,128]{1,0:T(8,128)S(1)}, u32[]{:S(2)}, u32[]{:S(2)}) %collective-permute-start.8) | collective-permute-done | bytes 917536 | tf_op jit(solution)/shard_map/ppermute | solution.py:62
  35.8 1.3 %collective-permute-start.10 = (f32[1792,128]{1,0:T(8,128)S(1)}, f32[1792,128]{1,0:T(8,128)S(1)}, u32[]{:S(2)}, u32[]{:S(2)}) collective-permute-start(f32[1792,128]{1,0:T(8,128)S(1)} %collective-permute-done.8.refs_1_), channel_id=1, source_target_pairs={{0,1},{1,0},{2,3},{3,2},{4,5},{5,4},{6,7},{7,6},{8,9},{9,8},{10,11... | collective-permute-start | bytes 2752520 | tf_op jit(solution)/shard_map/ppermute | solution.py:62
  37.2 0.0 collective-permute-start.12
  37.2 3.6 %collective-permute-done.11.refs_1_ = f32[896,128]{1,0:T(8,128)S(1)} collective-permute-done((f32[896,128]{1,0:T(8,128)S(1)}, f32[896,128]{1,0:T(8,128)S(1)}, u32[]{:S(2)}, u32[]{:S(2)}) %collective-permute-start.11) | collective-permute-done | bytes 458784 | tf_op jit(solution)/shard_map/ppermute | solution.py:62
  40.7 1.3 %collective-permute-start.13 = (f32[896,128]{1,0:T(8,128)S(1)}, f32[896,128]{1,0:T(8,128)S(1)}, u32[]{:S(2)}, u32[]{:S(2)}) collective-permute-start(f32[896,128]{1,0:T(8,128)S(1)} %collective-permute-done.11.refs_1_), channel_id=1, source_target_pairs={{0,1},{1,0},{2,3},{3,2},{4,5},{5,4},{6,7},{7,6},{8,9},{9,8},{10,11... | collective-permute-start | bytes 1376264 | tf_op jit(solution)/shard_map/ppermute | solution.py:62
  42.1 0.0 collective-permute-done.2.refs_0_
  42.1 1.2 %collective-permute-start.3 = (f32[896,128]{1,0:T(8,128)S(1)}, f32[896,128]{1,0:T(8,128)S(1)}, u32[]{:S(2)}, u32[]{:S(2)}) collective-permute-start(f32[896,128]{1,0:T(8,128)S(1)} %collective-permute-done.2.refs_0_), channel_id=1, source_target_pairs={{0,2},{1,5},{2,0},{3,7},{4,6},{5,1},{6,4},{7,3},{8,10},{9,13},{10,... | collective-permute-start | bytes 1376264 | tf_op jit(solution)/shard_map/ppermute | solution.py:62
  43.3 4.6 %plan.1 = (s32[4224]{0:T(1024)S(1)}, s32[8]{0:T(128)S(1)}) custom-call(s32[1,256]{1,0:T(1,128)} %bitcast.11, s32[4,256]{1,0:T(4,128)} %bitcast.10, s32[1,256]{1,0:T(1,128)} %bitcast.12), custom_call_target="tpu_custom_call" | custom-call | flops 1000000000 | bytes 1000000 | tf_op jit(solution)/shard_map/plan/pallas_call | solution.py:330
  47.9 4.4 %prep.1.at_ref = bf16[16384,96]{1,0:T(8,128)(2,1)S(1)} custom-call(f32[2,32768]{1,0:T(2,128)S(1)} %copy-done, f32[256,128]{1,0:T(8,128)S(1)} %bitcast.7), custom_call_target="tpu_custom_call" | custom-call | flops 4000000000 | bytes 10000000 | tf_op jit(solution)/shard_map/prep/pallas_call | solution.py:342
  52.3 0.1 collective-permute-start.4
  52.4 0.0 collective-permute-done.3.refs_1_
  52.4 0.5 collective-permute-start.5
  52.9 0.0 collective-permute-done.13.refs_3_
  52.9 9.2 %shard_map.104.refs_4_ = f32[257,8,128]{2,1,0:T(8,128)S(1)} custom-call(s32[4224]{0:T(1024)S(1)} %get-tuple-element.6.codes_ref, s32[8]{0:T(128)S(1)} %get-tuple-element.7.count_ref, bf16[16384,96]{1,0:T(8,128)(2,1)S(1)} %prep.1.at_ref, f32[896,128]{1,0:T(8,128)S(1)} %constant_dynamic-update-slice_fusion.refs_0_, ...), custom_call_target="tpu_custom_call" | custom-call | flops 4000000000 | bytes 10000000 | tf_op jit(solution)/shard_map/pallas_call | solution.py:281
  62.1 0.0 collective-permute-done.10.refs_3_
  62.2 13.3 %shard_map.105.refs_4_ = f32[257,8,128]{2,1,0:T(8,128)S(1)} custom-call(s32[4224]{0:T(1024)S(1)} %get-tuple-element.6.codes_ref, s32[8]{0:T(128)S(1)} %get-tuple-element.7.count_ref, bf16[16384,96]{1,0:T(8,128)(2,1)S(1)} %prep.1.at_ref, f32[1792,128]{1,0:T(8,128)S(1)} %constant_dynamic-update-slice_fusion.2.refs_0_, ...), custom_call_target="tpu_custom_call", output_to_operand_aliasing={{}: (7, {})} | custom-call | flops 4000000000 | bytes 10000000 | tf_op jit(solution)/shard_map/pallas_call | solution.py:281
  75.5 0.0 collective-permute-done.5.refs_3_
  75.5 10.8 %shard_map.106 = (f32[5,32768]{1,0:T(8,128)}, f32[256,128]{1,0:T(8,128)}) custom-call(s32[4224]{0:T(1024)S(1)} %get-tuple-element.6.codes_ref, s32[8]{0:T(128)S(1)} %get-tuple-element.7.count_ref, bf16[16384,96]{1,0:T(8,128)(2,1)S(1)} %prep.1.at_ref, f32[896,128]{1,0:T(8,128)S(1)} %collective-permute-done.2.refs_0_, ...), custom_call_target="tpu_custom_call" | custom-call | flops 4000000000 | bytes 10000000 | tf_op jit(solution)/shard_map/pallas_call | solution.py:281
  (13 shorter events, 0.1 us)
Async XLA Ops:
  1.8 5.8 %collective-permute-start.6 = (f32[448,128]{1,0:T(8,128)S(1)}, f32[448,128]{1,0:T(8,128)S(1)}, u32[]{:S(2)}, u32[]{:S(2)}) collective-permute-start(f32[448,128]{1,0:T(8,128)S(1)} %reshape.14), channel_id=1, source_target_pairs={{0,4},{1,3},{2,6},{3,1},{4,0},{5,7},{6,2},{7,5},{8,12},{9,11},{10,... | collective-permute-start | bytes 688136 | tf_op jit(solution)/shard_map/ppermute | solution.py:62
  4.0 8.2 %collective-permute-start = (f32[448,128]{1,0:T(8,128)S(1)}, f32[448,128]{1,0:T(8,128)S(1)}, u32[]{:S(2)}, u32[]{:S(2)}) collective-permute-start(f32[448,128]{1,0:T(8,128)S(1)} %reshape.14), channel_id=1, source_target_pairs={{0,8},{1,9},{2,10},{3,11},{4,12},{5,13},{6,14},{7,15},{8,16},{9,17... | collective-permute-start | bytes 688136 | tf_op jit(solution)/shard_map/ppermute | solution.py:62
  7.7 15.5 %collective-permute-start.7 = (f32[896,128]{1,0:T(8,128)S(1)}, f32[896,128]{1,0:T(8,128)S(1)}, u32[]{:S(2)}, u32[]{:S(2)}) collective-permute-start(f32[896,128]{1,0:T(8,128)S(1)} %constant_dynamic-update-slice_fusion.refs_0_), channel_id=1, source_target_pairs={{0,24},{1,25},{2,26},{3,27},{4,28},{5,29},{6,30},{7,31},{8,0},{9,1... | collective-permute-start | bytes 1376264 | tf_op jit(solution)/shard_map/ppermute | solution.py:62
  12.1 5.2 %collective-permute-start.1 = (f32[448,128]{1,0:T(8,128)S(1)}, f32[448,128]{1,0:T(8,128)S(1)}, u32[]{:S(2)}, u32[]{:S(2)}) collective-permute-start(f32[448,128]{1,0:T(8,128)S(1)} %collective-permute-done), channel_id=1, source_target_pairs={{0,4},{1,3},{2,6},{3,1},{4,0},{5,7},{6,2},{7,5},{8,12},{9,11},{10,... | collective-permute-start | bytes 688136 | tf_op jit(solution)/shard_map/ppermute | solution.py:62
  23.2 12.6 %collective-permute-start.8 = (f32[1792,128]{1,0:T(8,128)S(1)}, f32[1792,128]{1,0:T(8,128)S(1)}, u32[]{:S(2)}, u32[]{:S(2)}) collective-permute-start(f32[1792,128]{1,0:T(8,128)S(1)} %constant_dynamic-update-slice_fusion.2.refs_0_), channel_id=1, source_target_pairs={{0,2},{1,5},{2,0},{3,7},{4,6},{5,1},{6,4},{7,3},{8,10},{9,13},{10,... | collective-permute-start | bytes 2752520 | tf_op jit(solution)/shard_map/ppermute | solution.py:62
  24.5 16.2 %collective-permute-start.11 = (f32[896,128]{1,0:T(8,128)S(1)}, f32[896,128]{1,0:T(8,128)S(1)}, u32[]{:S(2)}, u32[]{:S(2)}) collective-permute-start(f32[896,128]{1,0:T(8,128)S(1)} %constant_dynamic-update-slice_fusion.refs_0_), channel_id=1, source_target_pairs={{0,2},{1,5},{2,0},{3,7},{4,6},{5,1},{6,4},{7,3},{8,10},{9,13},{10,... | collective-permute-start | bytes 1376264 | tf_op jit(solution)/shard_map/ppermute | solution.py:62
  24.8 17.3 %collective-permute-start.2 = (f32[896,128]{1,0:T(8,128)S(1)}, f32[896,128]{1,0:T(8,128)S(1)}, u32[]{:S(2)}, u32[]{:S(2)}) collective-permute-start(f32[896,128]{1,0:T(8,128)S(1)} %pad_maximum_fusion), channel_id=1, source_target_pairs={{0,8},{1,9},{2,10},{3,11},{4,12},{5,13},{6,14},{7,15},{8,16},{9,17... | collective-permute-start | bytes 1376264 | tf_op jit(solution)/shard_map/ppermute | solution.py:62
  24.8 37.3 %collective-permute-start.9 = (f32[1792,128]{1,0:T(8,128)S(1)}, f32[1792,128]{1,0:T(8,128)S(1)}, u32[]{:S(2)}, u32[]{:S(2)}) collective-permute-start(f32[1792,128]{1,0:T(8,128)S(1)} %constant_dynamic-update-slice_fusion.2.refs_0_), channel_id=1, source_target_pairs={{0,1},{1,0},{2,3},{3,2},{4,5},{5,4},{6,7},{7,6},{8,9},{9,8},{10,11... | collective-permute-start | bytes 2752520 | tf_op jit(solution)/shard_map/ppermute | solution.py:62
  35.8 26.3 %collective-permute-start.10 = (f32[1792,128]{1,0:T(8,128)S(1)}, f32[1792,128]{1,0:T(8,128)S(1)}, u32[]{:S(2)}, u32[]{:S(2)}) collective-permute-start(f32[1792,128]{1,0:T(8,128)S(1)} %collective-permute-done.8.refs_1_), channel_id=1, source_target_pairs={{0,1},{1,0},{2,3},{3,2},{4,5},{5,4},{6,7},{7,6},{8,9},{9,8},{10,11... | collective-permute-start | bytes 2752520 | tf_op jit(solution)/shard_map/ppermute | solution.py:62
  37.2 15.2 %collective-permute-start.12 = (f32[896,128]{1,0:T(8,128)S(1)}, f32[896,128]{1,0:T(8,128)S(1)}, u32[]{:S(2)}, u32[]{:S(2)}) collective-permute-start(f32[896,128]{1,0:T(8,128)S(1)} %constant_dynamic-update-slice_fusion.refs_0_), channel_id=1, source_target_pairs={{0,1},{1,0},{2,3},{3,2},{4,5},{5,4},{6,7},{7,6},{8,9},{9,8},{10,11... | collective-permute-start | bytes 1376264 | tf_op jit(solution)/shard_map/ppermute | solution.py:62
  40.7 12.2 %collective-permute-start.13 = (f32[896,128]{1,0:T(8,128)S(1)}, f32[896,128]{1,0:T(8,128)S(1)}, u32[]{:S(2)}, u32[]{:S(2)}) collective-permute-start(f32[896,128]{1,0:T(8,128)S(1)} %collective-permute-done.11.refs_1_), channel_id=1, source_target_pairs={{0,1},{1,0},{2,3},{3,2},{4,5},{5,4},{6,7},{7,6},{8,9},{9,8},{10,11... | collective-permute-start | bytes 1376264 | tf_op jit(solution)/shard_map/ppermute | solution.py:62
  42.1 10.3 %collective-permute-start.3 = (f32[896,128]{1,0:T(8,128)S(1)}, f32[896,128]{1,0:T(8,128)S(1)}, u32[]{:S(2)}, u32[]{:S(2)}) collective-permute-start(f32[896,128]{1,0:T(8,128)S(1)} %collective-permute-done.2.refs_0_), channel_id=1, source_target_pairs={{0,2},{1,5},{2,0},{3,7},{4,6},{5,1},{6,4},{7,3},{8,10},{9,13},{10,... | collective-permute-start | bytes 1376264 | tf_op jit(solution)/shard_map/ppermute | solution.py:62
  43.3 4.6 %copy-start = (f32[2,32768]{1,0:T(2,128)S(1)}, f32[2,32768]{1,0:T(2,128)}, u32[]{:S(2)}) copy-start(f32[2,32768]{1,0:T(2,128)} %coord_ref.1) | copy-start | bytes 786436
  43.3 4.6 %copy-start.1 = (f32[32768]{0:T(1024)S(1)}, f32[32768]{0:T(1024)}, u32[]{:S(2)}) copy-start(f32[32768]{0:T(1024)} %param.10) | copy-start | bytes 393220
  52.3 23.1 %collective-permute-start.4 = (f32[896,128]{1,0:T(8,128)S(1)}, f32[896,128]{1,0:T(8,128)S(1)}, u32[]{:S(2)}, u32[]{:S(2)}) collective-permute-start(f32[896,128]{1,0:T(8,128)S(1)} %collective-permute-done.2.refs_0_), channel_id=1, source_target_pairs={{0,1},{1,0},{2,3},{3,2},{4,5},{5,4},{6,7},{7,6},{8,9},{9,8},{10,11... | collective-permute-start | bytes 1376264 | tf_op jit(solution)/shard_map/ppermute | solution.py:62
  52.4 23.1 %collective-permute-start.5 = (f32[896,128]{1,0:T(8,128)S(1)}, f32[896,128]{1,0:T(8,128)S(1)}, u32[]{:S(2)}, u32[]{:S(2)}) collective-permute-start(f32[896,128]{1,0:T(8,128)S(1)} %collective-permute-done.3.refs_1_), channel_id=1, source_target_pairs={{0,1},{1,0},{2,3},{3,2},{4,5},{5,4},{6,7},{7,6},{8,9},{9,8},{10,11... | collective-permute-start | bytes 1376264 | tf_op jit(solution)/shard_map/ppermute | solution.py:62
